TPU v7x, 32 devices: a whole 2x2x4 slice. The times are simulated.
32 devices in a mesh: facet: 8 (over y, x, core), dp: 4 (over z).
Axes of the slice: x: 2, y: 2, z: 4, core: 2. Of those that a mesh axis runs over, the one named last changes fastest.
Arguments:
- sky_image: float32 [64, 512, 256], P('dp', 'facet'), as said below
- wave_dual: float32 [64, 512, 256], P('dp', 'facet'), may hold values from -3 to 3
- rank_dual: float32 [64, 512, 256], P('dp', 'facet'), may hold values from -3 to 3
- data_dual: float32 [8, 8, 1024, 256], P('facet', 'dp'), may hold values from -3 to 3
- observed: bfloat16 [8, 8, 1024, 256], P('facet', 'dp'), may hold values from -6 to 6
- radius: float32 [8, 8, 256], P('facet', 'dp'), may hold values from 20 to 400
- degrid: bfloat16 [8, 8, 24, 1024, 128], P('facet', 'dp'), may hold values from -0.15625 to 0.15625
- tile_list: int32 [8, 8, 24], P(None, 'dp'), may hold values from 0 to 63, as said below
- counts: int32 [8, 8], P(None, 'dp'), may hold values from 6 to 24
- keep_count: int32 [8], P('facet'), may hold values from 2 to 64
Outputs:
- sky_next: float32 [64, 512, 256], P('dp', 'facet')
- wave_next: float32 [64, 512, 256], P('dp', 'facet')
- rank_next: float32 [64, 512, 256], P('dp', 'facet')
- data_next: float32 [8, 8, 1024, 256], P('facet', 'dp')
Inputs may be any that keep to these rules, and one draw needn't show every extreme that they name: `sky_image`: nonnegative. `tile_list`: A slot's value is f * 8 + t, tile t of source facet f in the block's band. Among the live slots of the 2 blocks of one device (facet g, band d) at most 6 name one source facet; in every band some source facet is named by exactly 6 live slots of every device of that band.
All inputs are finite; a program needn't handle non-finite values.
Results may differ from a plain program's by a relative error of at most 0.005.
Values may be sent and summed in bfloat16 or wider, within the bound.
No kernel may reach another device: no remote copies, remote signals or barrier semaphores. Data moves between devices by JAX's collectives and lax.ppermute only.
A program may use at most 128 MiB of HBM per device.

v0:
```python
import functools

import jax
import jax.numpy as jnp
from jax import lax
from jax.experimental import pallas as pl
from jax.experimental.pallas import tpu as pltpu
from jax.sharding import PartitionSpec as P


TR = 8
TC = 16
MIB = 1 << 20


wavelet_taps = (-0.12940952255126037, -0.2241438680420134, 0.8365163037378079, -0.48296291314453416)
step_primal = 0.5
step_wave = 0.5
wave_bound = 1.0
step_rank = 0.5

any_spec = pl.BlockSpec(memory_space=pl.ANY)
smem_spec = pl.BlockSpec(memory_space=pltpu.SMEM)
hbm_spec = pl.BlockSpec(memory_space=pltpu.HBM)
vmem_spec = pl.BlockSpec(memory_space=pltpu.VMEM)
adjoint_group = 8
forward_group = 8


def in_hbm(value):
    return pltpu.with_memory_space_constraint(value, pltpu.HBM)


def swap(value, axis, mask):
    count = lax.axis_size(axis)
    return lax.ppermute(value, axis, [(i, i ^ mask) for i in range(count)])


def padded_2(block, sides, width):
    for axis, dim, even in sides:
        count = lax.axis_size(axis)
        outer = [(i, i + 1) for i in range(1, count - 1, 2)]
        outer = outer + [(target, source) for source, target in outer]
        first = lax.slice_in_dim(block, 0, width, axis=dim)
        last = lax.slice_in_dim(block, block.shape[dim] - width, None, axis=dim)
        inward = jnp.where(even, last, first)
        outward = jnp.where(even, first, last)
        inside = swap(inward, axis, 1)
        outside = lax.ppermute(outward, axis, outer)
        low = jnp.where(even, outside, inside)
        high = jnp.where(even, inside, outside)
        block = jnp.concatenate([low, block, high], axis=dim)
    return block


def analysis(padded, height, columns):
    across = sum(
        (
            wavelet_taps[offset] * padded[offset + 1 : offset + 1 + height, :, :]
            for offset in range(4)
        )
    )
    return sum(
        (
            wavelet_taps[offset] * across[:, offset + 1 : offset + 1 + columns, :]
            for offset in range(4)
        )
    )


def synthesis(padded, height, columns):
    across = sum(
        (
            wavelet_taps[offset] * padded[3 - offset : 3 - offset + height, :, :]
            for offset in range(4)
        )
    )
    return sum(
        (
            wavelet_taps[offset] * across[:, 3 - offset : 3 - offset + columns, :]
            for offset in range(4)
        )
    )


def slot_chunks(degrid_hbm, buf, sems, group):
    blocks, depth = degrid_hbm.shape[1:3]
    return [
        [
            pltpu.make_async_copy(
                degrid_hbm.at[0, b, pl.ds(c * group, group)],
                buf.at[b, pl.ds(c * group, group)],
                sems.at[b, c],
            )
            for c in range(depth // group)
        ]
        for b in range(blocks)
    ]


def relative_tile(tiles, me, block, slot, count, tile_count, dummy):
    tile = tiles[me, block, jnp.minimum(slot, count - 1)]
    source = lax.div(tile, tile_count)
    place = lax.bitwise_xor(source, me) * tile_count + (tile - source * tile_count)
    return jnp.where(slot < count, place, dummy)


def adjoint_body(
    tiles_hbm, counts_hbm, dual_hbm, degrid_hbm,
    even_far_ref, even_mid_ref, even_own_ref, odd_far_ref, odd_mid_ref, odd_own_ref,
    tiles, counts, dual, turned, acc, buf, sems, dual_sems, list_sems,
    *, chips, tile_count, group,
):
    blocks, depth = degrid_hbm.shape[1:3]
    pixels = degrid_hbm.shape[4]
    me = lax.axis_index("facet")
    chunks = slot_chunks(degrid_hbm, buf, sems, group)
    lists = [
        pltpu.make_async_copy(counts_hbm, counts, list_sems.at[0]),
        pltpu.make_async_copy(tiles_hbm, tiles, list_sems.at[1]),
    ]
    duals = [
        pltpu.make_async_copy(dual_hbm.at[0, b], dual.at[b], dual_sems.at[b]) for b in range(blocks)
    ]
    for copy in lists + duals:
        copy.start()
    for b in range(blocks):
        chunks[b][0].start()
    for copy in lists:
        copy.wait()
    for b in range(blocks):
        for c in range(1, depth // group):
            @pl.when(c * group < counts[b, me])
            def _():
                chunks[b][c].start()
    live = 2 * chips * tile_count
    acc[...] = jnp.zeros_like(acc)
    for b in range(blocks):
        duals[b].wait()
        turned[b] = dual[b].astype(jnp.bfloat16).T
    for b in range(blocks):
        for c in range(depth // group):
            @pl.when(c * group < counts[b, me])
            def _():
                chunks[b][c].wait()
                right = jnp.concatenate([buf[b, c * group + j] for j in range(group)], axis=1)
                result = jnp.dot(turned[b], right, preferred_element_type=jnp.float32)
                result = result.astype(jnp.bfloat16).astype(jnp.float32)
                for j in range(group):
                    name = relative_tile(
                        tiles, me, b, c * group + j, counts[b, me], tile_count, live
                    )
                    acc[name] = acc[name] + result[:, j * pixels : (j + 1) * pixels]

    for k in range(chips):
        first = 2 * k * tile_count
        even = acc[first : first + tile_count].astype(jnp.bfloat16)
        odd = acc[first + tile_count : first + 2 * tile_count].astype(jnp.bfloat16)
        if k == chips - 1:
            even_far_ref[...] = even
            odd_far_ref[...] = odd
        elif k:
            even_mid_ref[k - 1] = even
            odd_mid_ref[k - 1] = odd
        else:
            even_own_ref[...] = even
            odd_own_ref[...] = odd


def adjoint(tile_list, counts, dual, degrid, chips, tile_count):
    _, blocks, depth, entries, pixels = degrid.shape
    channels = dual.shape[-1]
    group = adjoint_group

    def tiles_of(*lead):
        return jax.ShapeDtypeStruct(lead + (tile_count, channels, pixels), jnp.bfloat16)

    return pl.pallas_call(
        functools.partial(adjoint_body, chips=chips, tile_count=tile_count, group=group),
        out_shape=[tiles_of(), tiles_of(chips - 2), tiles_of()] * 2,
        in_specs=[hbm_spec] * 4,
        out_specs=[vmem_spec] * 6,
        scratch_shapes=[
            pltpu.SMEM(tile_list.shape, jnp.int32),
            pltpu.SMEM(counts.shape, jnp.int32),
            pltpu.VMEM((blocks, entries, channels), jnp.float32),
            pltpu.VMEM((blocks, channels, entries), jnp.bfloat16),
            pltpu.VMEM((2 * chips * tile_count + 1, channels, pixels), jnp.float32),
            pltpu.VMEM((blocks, depth, entries, pixels), jnp.bfloat16),
            pltpu.SemaphoreType.DMA((blocks, depth // group)),
            pltpu.SemaphoreType.DMA((blocks,)),
            pltpu.SemaphoreType.DMA((2,)),
        ],
        compiler_params=pltpu.CompilerParams(vmem_limit_bytes=(30 if chips == 4 else 50) * MIB),
        name="adjoint",
    )(*(in_hbm(value) for value in (tile_list, counts, dual, degrid)))


def primal_body(*refs, parts):
    sky_ref, rest_ref, own_ref, mate_ref = refs[:4]
    halves = (refs[4 : 4 + parts], refs[4 + parts : 4 + 2 * parts])
    next_ref, extrap_ref = refs[4 + 2 * parts : 6 + 2 * parts]
    tiles_ref = refs[6 + 2 * parts]
    _, columns, channels = sky_ref.shape
    across = columns // TC
    half = tiles_ref.shape[0] // 2
    for h in range(2):
        for t in range(half):
            tile = h * half + t
            total = own_ref[tile].astype(jnp.float32) + mate_ref[tile].astype(jnp.float32)
            for part in halves[h]:
                total = total + part[t].astype(jnp.float32)
            back = total.T.reshape(TR, TC, channels)
            rows = pl.ds(tile // across * TR, TR)
            cols = pl.ds(tile % across * TC, TC)
            sky = sky_ref[rows, cols, :]
            new = jnp.maximum(sky - step_primal * (back + rest_ref[rows, cols, :]), 0.0)
            extrap = 2.0 * new - sky
            next_ref[rows, cols, :] = new
            extrap_ref[rows, cols, :] = extrap
            tiles_ref[tile] = extrap.reshape(TR * TC, channels).astype(jnp.bfloat16)


def primal(sky, rest, own, mate, low, high):
    whole = jax.ShapeDtypeStruct(sky.shape, jnp.float32)
    tiles = jax.ShapeDtypeStruct((own.shape[0], own.shape[2], own.shape[1]), jnp.bfloat16)
    return pl.pallas_call(
        functools.partial(primal_body, parts=len(low)),
        out_shape=[whole, whole, tiles],
        in_specs=[vmem_spec] * (4 + len(low) + len(high)),
        out_specs=[vmem_spec] * 3,
        compiler_params=pltpu.CompilerParams(vmem_limit_bytes=24 * MIB),
        name="primal",
    )(sky, rest, own, mate, *low, *high)


def gram_body(extrap_ref, rank_ref, packed_ref):
    height, columns, channels = extrap_ref.shape
    half = channels // 2
    mixed = (rank_ref[...] + step_rank * extrap_ref[...]).reshape(height * columns, channels)
    gram = lax.dot_general(
        mixed, mixed, (((0,), (0,)), ((), ())),
        precision=lax.Precision.HIGHEST, preferred_element_type=jnp.float32,
    )
    row = lax.broadcasted_iota(jnp.int32, (half, half), 0)
    col = lax.broadcasted_iota(jnp.int32, (half, half), 1)
    corner = gram[half:, half:]
    packed_ref[0:half] = jnp.where(col >= row, gram[:half, :half], corner)
    packed_ref[half:channels] = gram[:half, half:]
    packed_ref[channels:] = jnp.broadcast_to(
        jnp.sum(jnp.where(col == row, corner, 0.0), axis=0, keepdims=True), (8, half)
    )


def gram_of(extrap, rank_dual):
    channels = extrap.shape[2]
    return pl.pallas_call(
        gram_body,
        out_shape=jax.ShapeDtypeStruct((channels + 8, channels // 2), jnp.float32),
        in_specs=[vmem_spec, vmem_spec],
        out_specs=vmem_spec,
        compiler_params=pltpu.CompilerParams(vmem_limit_bytes=24 * MIB),
        name="gram",
    )(extrap, rank_dual)


def split(value):
    high = value.astype(jnp.bfloat16)
    return high, (value - high.astype(jnp.float32)).astype(jnp.bfloat16)


def dot_fine(left, right):
    a, b = split(left)
    c, d = split(right)
    return (
        jnp.dot(a, c, preferred_element_type=jnp.float32)
        + jnp.dot(a, d, preferred_element_type=jnp.float32)
        + jnp.dot(b, c, preferred_element_type=jnp.float32)
    )


def dot_full(left, right):
    return jnp.dot(
        left, right, precision=lax.Precision.HIGHEST, preferred_element_type=jnp.float32
    )


def dot_quick(left, right):
    return jnp.dot(
        left.astype(jnp.bfloat16), right.astype(jnp.bfloat16), preferred_element_type=jnp.float32
    )


def rank_body(keep_ref, *refs, parts):
    packed_refs = refs[:parts]
    extrap_hbm, rank_hbm, out_ref, extrap_buf, rank_buf, sems = refs[parts:]
    loads = [
        pltpu.make_async_copy(extrap_hbm, extrap_buf, sems.at[0]),
        pltpu.make_async_copy(rank_hbm, rank_buf, sems.at[1]),
    ]
    for load in loads:
        load.start()
    height, columns, channels = extrap_buf.shape
    half = channels // 2
    packed = packed_refs[0][...]
    for ref in packed_refs[1:]:
        packed = packed + ref[...]
    row = lax.broadcasted_iota(jnp.int32, (half, half), 0)
    col = lax.broadcasted_iota(jnp.int32, (half, half), 1)
    mix = packed[:half]
    upper = jnp.where(col > row, mix, 0.0)
    lower = jnp.where(col < row, mix, 0.0)
    first = jnp.where(col >= row, mix, 0.0) + upper.T
    tail = packed[channels : channels + 1]
    last = lower + lower.T + jnp.where(col == row, jnp.broadcast_to(tail, (half, half)), 0.0)
    cross = packed[half:channels]
    gram = jnp.concatenate(
        [jnp.concatenate([first, cross], axis=1), jnp.concatenate([cross.T, last], axis=1)], axis=0
    )
    wide_row = lax.broadcasted_iota(jnp.int32, (channels, channels), 0)
    wide_col = lax.broadcasted_iota(jnp.int32, (channels, channels), 1)
    eye = jnp.where(wide_row == wide_col, 1.0, 0.0).astype(jnp.float32)
    keep = jnp.full((1, 1), keep_ref[0], jnp.int32).astype(jnp.float32)
    trace = jnp.sum(jnp.sum(gram * eye, axis=0, keepdims=True), axis=1, keepdims=True)
    level = (trace + 1e-06) / keep
    system = gram / level + eye
    scale = 2.0 / (2.0 + keep)
    error = eye - scale * system
    inverse = scale * (eye + error)
    error = dot_quick(error, error)
    for step in range(6):
        if step < 5:
            both = dot_quick(jnp.concatenate([inverse, error], axis=0), error)
            inverse = inverse + both[:channels]
            error = both[channels:]
        else:
            inverse = inverse + dot_quick(inverse, error)
    for _ in range(2):
        residual = eye - dot_fine(system, inverse)
        inverse = inverse + dot_fine(inverse, residual)
    residual = eye - dot_full(system, inverse)
    inverse = inverse + dot_fine(inverse, residual)
    for load in loads:
        load.wait()
    mixed = (rank_buf[...] + step_rank * extrap_buf[...]).reshape(height * columns, channels)
    out_ref[...] = dot_fine(mixed, inverse).reshape(height, columns, channels)


def rank_update(keep_count, packed, extrap, rank_dual):
    return pl.pallas_call(
        functools.partial(rank_body, parts=len(packed)),
        out_shape=jax.ShapeDtypeStruct(extrap.shape, jnp.float32),
        in_specs=[smem_spec] + [vmem_spec] * len(packed) + [any_spec, any_spec],
        out_specs=vmem_spec,
        scratch_shapes=[
            pltpu.VMEM(extrap.shape, jnp.float32),
            pltpu.VMEM(extrap.shape, jnp.float32),
            pltpu.SemaphoreType.DMA((2,)),
        ],
        compiler_params=pltpu.CompilerParams(vmem_limit_bytes=32 * MIB),
        name="rank",
    )(keep_count, *packed, extrap, rank_dual)


def forward_body(
    tiles_hbm, counts_hbm, degrid_hbm, dual_hbm, seen_hbm, radius_ref, *refs,
    chips, tile_count, group,
):
    held = 2 * chips
    image_refs, out_hbm = refs[:held], refs[held]
    tiles, counts, dual, seen, image, acc, buf, sems, image_sems, wide_sems, list_sems = refs[
        held + 1 :
    ]
    blocks, depth, _, _ = degrid_hbm.shape[1:5]
    me = lax.axis_index("facet")
    chunks = slot_chunks(degrid_hbm, buf, sems, group)
    lists = [
        pltpu.make_async_copy(counts_hbm, counts, list_sems.at[0]),
        pltpu.make_async_copy(tiles_hbm, tiles, list_sems.at[1]),
    ]
    images = [
        pltpu.make_async_copy(
            image_refs[i], image.at[pl.ds(i * tile_count, tile_count)], image_sems.at[i]
        )
        for i in range(held)
    ]
    wide = [
        pltpu.make_async_copy(dual_hbm.at[0], dual, wide_sems.at[0]),
        pltpu.make_async_copy(seen_hbm.at[0], seen, wide_sems.at[1]),
    ]
    stores = [
        pltpu.make_async_copy(acc.at[b], out_hbm.at[0, b], wide_sems.at[2 + b]) for b in range(blocks)
    ]
    for copy in lists:
        copy.start()
    chunks[0][0].start()
    for copy in images:
        copy.start()
    for b in range(1, blocks):
        chunks[b][0].start()
    for copy in lists:
        copy.wait()
    for b in range(blocks):
        for c in range(1, depth // group):
            @pl.when(c * group < counts[b, me])
            def _():
                chunks[b][c].start()
        if b == 0:
            for copy in wide:
                copy.start()
    live = held * tile_count
    image[live] = jnp.zeros_like(image[live])
    for copy in images:
        copy.wait()
    for b in range(blocks):
        for c in range(depth // group):
            @pl.when(c * group < counts[b, me])
            def _():
                chunks[b][c].wait()
                names = [
                    relative_tile(tiles, me, b, c * group + j, counts[b, me], tile_count, live)
                    for j in range(group)
                ]
                left = jnp.concatenate([buf[b, c * group + j] for j in range(group)], axis=1)
                right = jnp.concatenate([image[name] for name in names], axis=0)
                product = jnp.dot(left, right, preferred_element_type=jnp.float32)
                acc[b] = acc[b] + product if c else product

        if b == 0:
            for copy in wide:
                copy.wait()
        misfit = acc[b] + (dual[b] - seen[b].astype(jnp.float32))
        size = jnp.sqrt(jnp.sum(misfit * misfit, axis=0, keepdims=True) + 1e-06)
        scale = jnp.maximum(0.0, 1.0 - radius_ref[0, b : b + 1, :] / size)
        acc[b] = misfit * scale
        stores[b].start()
    for copy in stores:
        copy.wait()


def forward(tile_list, counts, degrid, dual, observed, radius, image, chips, tile_count):
    _, blocks, depth, entries, pixels = degrid.shape
    channels = dual.shape[-1]
    group = forward_group
    return pl.pallas_call(
        functools.partial(forward_body, chips=chips, tile_count=tile_count, group=group),
        out_shape=jax.ShapeDtypeStruct(dual.shape, jnp.float32),
        in_specs=[hbm_spec] * 5 + [vmem_spec] + [any_spec] * len(image),
        out_specs=hbm_spec,
        scratch_shapes=[
            pltpu.SMEM(tile_list.shape, jnp.int32),
            pltpu.SMEM(counts.shape, jnp.int32),
            pltpu.VMEM((blocks, entries, channels), jnp.float32),
            pltpu.VMEM((blocks, entries, channels), jnp.bfloat16),
            pltpu.VMEM((2 * chips * tile_count + 1, pixels, channels), jnp.bfloat16),
            pltpu.VMEM((blocks, entries, channels), jnp.float32),
            pltpu.VMEM((blocks, depth, entries, pixels), jnp.bfloat16),
            pltpu.SemaphoreType.DMA((blocks, depth // group)),
            pltpu.SemaphoreType.DMA((2 * chips,)),
            pltpu.SemaphoreType.DMA((2 + blocks,)),
            pltpu.SemaphoreType.DMA((2,)),
        ],
        compiler_params=pltpu.CompilerParams(vmem_limit_bytes=32 * MIB),
        name="forward",
    )(
        *(in_hbm(value) for value in (tile_list, counts, degrid, dual, observed)),
        radius,
        *image,
    )


def plus(*values):
    total = values[0].astype(jnp.float32)
    for value in values[1:]:
        total = total + value.astype(jnp.float32)
    return total.astype(jnp.bfloat16)


def to_owners(evens, odds, chips):
    even_far, even_mid, _ = evens
    half = even_far.shape[0] // 2
    far = swap(odds[0], "facet", 1)
    mid = swap(odds[1], "facet", 1)
    low, high = slice(0, half), slice(half, None)
    if chips == 4:
        via_x = swap(plus(even_far[low], far[low]), "facet", 2)
        via_y = swap(plus(even_far[high], far[high]), "facet", 4)
        x_low = swap(plus(even_mid[0, low], mid[0, low]), "facet", 2)
        y_high = swap(plus(even_mid[1, high], mid[1, high]), "facet", 4)
        own = swap(odds[2], "facet", 1)
        x_high = swap(plus(even_mid[0, high], mid[0, high], via_y), "facet", 2)
        y_low = swap(plus(even_mid[1, low], mid[1, low], via_x), "facet", 4)
        return own, [x_low, y_low], [x_high, y_high]
    own = swap(odds[2], "facet", 1)
    lows, highs = [], []
    for k in range(1, chips):
        pair = (even_far, far) if k == chips - 1 else (even_mid[k - 1], mid[k - 1])
        got = swap(plus(*pair), "facet", 2 * k)
        lows.append(got[low])
        highs.append(got[high])
    return own, lows, highs


def from_owners(tiles, chips):
    reached = [tiles]
    for k in range(1, chips):
        reached.append(swap(tiles, "facet", 2 * k))
    image = []
    for k in range(chips):
        image.append(reached[k])
        image.append(swap(reached[k], "facet", 1))
    return image


def per_device(
    sky_image,
    wave_dual,
    rank_dual,
    data_dual,
    observed,
    radius,
    degrid,
    tile_list,
    counts,
    keep_count,
):
    return iteration(
        sky_image,
        wave_dual,
        rank_dual,
        data_dual,
        observed,
        radius,
        degrid,
        tile_list,
        counts.T,
        keep_count,
    )


def iteration(
    sky_image,
    wave_dual,
    rank_dual,
    data_dual,
    observed,
    radius,
    degrid,
    tile_list,
    counts,
    keep_count,
):
    height, columns, _ = sky_image.shape
    facets = lax.axis_size("facet")
    chips = facets // 2
    tile_count = height // TR * (columns // TC)

    even_column = lax.rem(lax.axis_index("facet"), 2) == 0
    even_row = lax.rem(lax.axis_index("dp"), 2) == 0
    tile_list, even_column, even_row = lax.optimization_barrier((tile_list, even_column, even_row))
    sides = (("facet", 1, even_column), ("dp", 0, even_row))
    sums = adjoint(tile_list, counts, data_dual, degrid, chips, tile_count)
    mate_own, low, high = to_owners(sums[:3], sums[3:], chips)

    wave_halo = padded_2(wave_dual, sides, 2)
    rest = synthesis(wave_halo, height, columns) + rank_dual
    sky_next, extrap, tiles = primal(sky_image, rest, sums[2], mate_own, low, high)

    image = from_owners(tiles, chips)
    packed = gram_of(extrap, rank_dual)
    bar_halo = padded_2(extrap, sides, 2)
    wave_next = jnp.clip(
        wave_dual + step_wave * analysis(bar_halo, height, columns), -wave_bound, wave_bound
    )
    stride = 1
    got = swap(packed, "dp", 1)
    while 2 * stride < lax.axis_size("dp"):
        stride = 2 * stride
        packed = packed + got
        got = swap(packed, "dp", stride)
    rank_next = rank_update(keep_count, [packed, got], extrap, rank_dual)
    data_next = forward(
        tile_list, counts, degrid, data_dual, observed, radius, image, chips, tile_count
    )
    return (sky_next, wave_next, rank_next, data_next)


def solution(mesh):
    return jax.shard_map(
        per_device,
        mesh=mesh,
        in_specs=(
            P("dp", "facet", None),
            P("dp", "facet", None),
            P("dp", "facet", None),
            P("facet", "dp", None, None),
            P("facet", "dp", None, None),
            P("facet", "dp", None),
            P("facet", "dp", None, None, None),
            P(None, "dp", None),
            P(None, "dp"),
            P("facet"),
        ),
        out_specs=(
            P("dp", "facet", None),
            P("dp", "facet", None),
            P("dp", "facet", None),
            P("facet", "dp", None, None),
        ),
        check_vma=False,
    )
```

profile of v0, /device:TPU:10, one launch (start us, length us, event | category | flops | bytes accessed | tf_op | source)
XLA Modules:
  0.0 92.7 jit_solution(7191706373673854844)
XLA Ops:
  0.6 1.0 %broadcast_select_fusion.11 = (f32[16,2,256]{2,1,0:T(2,128)S(1)}, f32[16,2,256]{2,1,0:T(2,128)S(1)}) fusion(pred[]{:T(512)S(6)} %eq.6, f32[16,64,256]{2,1,0:T(8,128)} %param.11), kind=kLoop, calls=%fused_computation.65 | loop fusion | flops 16384 | bytes 131073 | tf_op jit(solution)/shard_map/jit(_where)/select_n | solution.py:47
  1.6 1.9 %collective-permute-start = (f32[16,2,256]{2,1,0:T(2,128)S(1)}, f32[16,2,256]{2,1,0:T(2,128)S(1)}, u32[]{:S(2)}, u32[]{:S(2)}) collective-permute-start(f32[16,2,256]{2,1,0:T(2,128)S(1)} %get-tuple-element.40), channel_id=1, source_target_pairs={{4,8},{12,16},{20,24},{8,4},{16,12},{24,20},{5,9},{13,17},{21,25},... | collective-permute-start | bytes 98312 | tf_op jit(solution)/shard_map/ppermute | solution.py:49
  3.6 1.7 %collective-permute-start.1 = (f32[16,2,256]{2,1,0:T(2,128)S(1)}, f32[16,2,256]{2,1,0:T(2,128)S(1)}, u32[]{:S(2)}, u32[]{:S(2)}) collective-permute-start(f32[16,2,256]{2,1,0:T(2,128)S(1)} %get-tuple-element.41), channel_id=1, source_target_pairs={{0,4},{4,0},{8,12},{12,8},{16,20},{20,16},{24,28},{28,24},{1,5},{5... | collective-permute-start | bytes 98312 | tf_op jit(solution)/shard_map/ppermute | solution.py:36
  5.2 8.1 %adjoint.1 = (bf16[8,256,128]{2,1,0:T(8,128)(2,1)S(1)}, bf16[2,8,256,128]{3,2,1,0:T(8,128)(2,1)S(1)}, bf16[8,256,128]{2,1,0:T(8,128)(2,1)S(1)}, bf16[8,256,128]{...) custom-call(s32[8,2,24]{2,1,0:T(2,128)} %tiles_hbm.1, s32[2,8]{1,0:T(2,128)} %bitcast.37, ...), custom_call_target="tpu_custom_call" | custom-call | tf_op jit(solution)/shard_map/adjoint/pallas_call | solution.py:178
  13.4 0.1 pad_maximum_fusion.7
  13.6 0.5 collective-permute-start.2
  14.1 3.1 %collective-permute-start.3 = (f32[2,68,256]{2,1,0:T(8,128)S(1)}, f32[2,68,256]{2,1,0:T(8,128)S(1)}, u32[]{:S(2)}, u32[]{:S(2)}) collective-permute-start(f32[2,68,256]{2,1,0:T(8,128)S(1)} %get-tuple-element.35), channel_id=1, source_target_pairs={{1,2},{2,1},{5,6},{6,5},{9,10},{10,9},{13,14},{14,13},{17,18},{18,... | collective-permute-start | bytes 417800 | tf_op jit(solution)/shard_map/ppermute | solution.py:49
  17.3 0.5 collective-permute-start.4
  17.8 2.1 %collective-permute-done.2 = f32[2,68,256]{2,1,0:T(8,128)S(1)} collective-permute-done((f32[2,68,256]{2,1,0:T(8,128)S(1)}, f32[2,68,256]{2,1,0:T(8,128)S(1)}, u32[]{:S(2)}, u32[]{:S(2)}) %collective-permute-start.2) | collective-permute-done | bytes 139296 | tf_op jit(solution)/shard_map/ppermute | solution.py:36
  19.9 1.9 %collective-permute-done.3 = f32[2,68,256]{2,1,0:T(8,128)S(1)} collective-permute-done((f32[2,68,256]{2,1,0:T(8,128)S(1)}, f32[2,68,256]{2,1,0:T(8,128)S(1)}, u32[]{:S(2)}, u32[]{:S(2)}) %collective-permute-start.3) | collective-permute-done | bytes 139296 | tf_op jit(solution)/shard_map/ppermute | solution.py:49
  21.8 0.1 maximum_maximum_fusion
  22.0 0.1 add_convert_fusion.1
  22.1 0.4 collective-permute-start.10
  22.5 2.9 %collective-permute-start.8 = (bf16[4,256,128]{2,1,0:T(8,128)(2,1)S(1)}, bf16[4,256,128]{2,1,0:T(8,128)(2,1)S(1)}, u32[]{:S(2)}, u32[]{:S(2)}) collective-permute-start(bf16[4,256,128]{2,1,0:T(8,128)(2,1)S(1)} %get-tuple-element.39), channel_id=1, source_target_pairs={{0,8},{4,12},{8,0},{12,4},{16,24},{20,28},{24,16},{28,20},{1,9},{5... | collective-permute-start | bytes 786440 | tf_op jit(solution)/shard_map/ppermute | solution.py:36
  25.4 0.4 fusion.4
  25.7 3.9 %collective-permute-done.10 = bf16[4,256,128]{2,1,0:T(8,128)(2,1)S(1)} collective-permute-done((bf16[4,256,128]{2,1,0:T(8,128)(2,1)S(1)}, bf16[4,256,128]{2,1,0:T(8,128)(2,1)S(1)}, u32[]{:S(2)}, u32[]{:S(2)}) %collective-permute-start.10) | collective-permute-done | bytes 262176 | tf_op jit(solution)/shard_map/ppermute | solution.py:36
  29.6 1.6 %collective-permute-done.8 = bf16[4,256,128]{2,1,0:T(8,128)(2,1)S(1)} collective-permute-done((bf16[4,256,128]{2,1,0:T(8,128)(2,1)S(1)}, bf16[4,256,128]{2,1,0:T(8,128)(2,1)S(1)}, u32[]{:S(2)}, u32[]{:S(2)}) %collective-permute-start.8) | collective-permute-done | bytes 262176 | tf_op jit(solution)/shard_map/ppermute | solution.py:36
  31.2 0.2 fusion.18
  31.4 1.8 %collective-permute-start.11 = (bf16[4,256,128]{2,1,0:T(8,128)(2,1)S(1)}, bf16[4,256,128]{2,1,0:T(8,128)(2,1)S(1)}, u32[]{:S(2)}, u32[]{:S(2)}) collective-permute-start(bf16[4,256,128]{2,1,0:T(8,128)(2,1)S(1)} %get-tuple-element.30), channel_id=1, source_target_pairs={{0,8},{4,12},{8,0},{12,4},{16,24},{20,28},{24,16},{28,20},{1,9},{5... | collective-permute-start | bytes 786440 | tf_op jit(solution)/shard_map/ppermute | solution.py:36
  33.2 0.4 collective-permute-start.9
  33.6 0.1 fusion.21
  33.7 1.7 %collective-permute-start.12 = (bf16[4,256,128]{2,1,0:T(8,128)(2,1)S(1)}, bf16[4,256,128]{2,1,0:T(8,128)(2,1)S(1)}, u32[]{:S(2)}, u32[]{:S(2)}) collective-permute-start(bf16[4,256,128]{2,1,0:T(8,128)(2,1)S(1)} %get-tuple-element.28), channel_id=1, source_target_pairs={{0,16},{4,20},{8,24},{12,28},{16,0},{20,4},{24,8},{28,12},{1,17},{... | collective-permute-start | bytes 786440 | tf_op jit(solution)/shard_map/ppermute | solution.py:36
  35.4 0.3 collective-permute-start.6
  35.7 0.5 fusion.15.refs_1_
  36.2 4.4 %collective-permute-done.11.refs_6_ = bf16[4,256,128]{2,1,0:T(8,128)(2,1)S(1)} collective-permute-done((bf16[4,256,128]{2,1,0:T(8,128)(2,1)S(1)}, bf16[4,256,128]{2,1,0:T(8,128)(2,1)S(1)}, u32[]{:S(2)}, u32[]{:S(2)}) %collective-permute-start.11) | collective-permute-done | bytes 262176 | tf_op jit(solution)/shard_map/ppermute | solution.py:36
  40.6 1.7 %collective-permute-done.9.refs_5_ = bf16[4,256,128]{2,1,0:T(8,128)(2,1)S(1)} collective-permute-done((bf16[4,256,128]{2,1,0:T(8,128)(2,1)S(1)}, bf16[4,256,128]{2,1,0:T(8,128)(2,1)S(1)}, u32[]{:S(2)}, u32[]{:S(2)}) %collective-permute-start.9) | collective-permute-done | bytes 262176 | tf_op jit(solution)/shard_map/ppermute | solution.py:36
  42.4 2.9 %collective-permute-done.12.refs_7_ = bf16[4,256,128]{2,1,0:T(8,128)(2,1)S(1)} collective-permute-done((bf16[4,256,128]{2,1,0:T(8,128)(2,1)S(1)}, bf16[4,256,128]{2,1,0:T(8,128)(2,1)S(1)}, u32[]{:S(2)}, u32[]{:S(2)}) %collective-permute-start.12) | collective-permute-done | bytes 262176 | tf_op jit(solution)/shard_map/ppermute | solution.py:36
  45.2 1.4 %primal.1 = (f32[16,64,256]{2,1,0:T(8,128)}, f32[16,64,256]{2,1,0:T(8,128)S(1)}, bf16[8,128,256]{2,1,0:T(8,128)(2,1)S(1)}) custom-call(f32[16,64,256]{2,1,0:T(8,128)S(1)} %copy-done.1, f32[16,64,256]{2,1,0:T(8,128)S(1)} %fusion.15.refs_1_, bf16[8,256,128]{2,1,0:T(8,128)(2,1)S(1)} %get-tuple-element.19.refs_2_, ...), custom_call_target="tpu_custom_call" | custom-call | tf_op jit(solution)/shard_map/primal/pallas_call | solution.py:227
  46.7 1.9 %collective-permute-start.13 = (f32[16,2,256]{2,1,0:T(2,128)S(1)}, f32[16,2,256]{2,1,0:T(2,128)S(1)}, u32[]{:S(2)}, u32[]{:S(2)}) collective-permute-start(f32[16,2,256]{2,1,0:T(2,128)S(1)} %get-tuple-element.36), channel_id=1, source_target_pairs={{4,8},{12,16},{20,24},{8,4},{16,12},{24,20},{5,9},{13,17},{21,25},... | collective-permute-start | bytes 98312 | tf_op jit(solution)/shard_map/ppermute | solution.py:49
  48.6 0.6 collective-permute-start.14
  49.2 1.6 %collective-permute-start.20 = (bf16[8,128,256]{2,1,0:T(8,128)(2,1)S(1)}, bf16[8,128,256]{2,1,0:T(8,128)(2,1)S(1)}, u32[]{:S(2)}, u32[]{:S(2)}) collective-permute-start(bf16[8,128,256]{2,1,0:T(8,128)(2,1)S(1)} %get-tuple-element.27.refs_0_), channel_id=1, source_target_pairs={{0,8},{4,12},{8,0},{12,4},{16,24},{20,28},{24,16},{28,20},{1,9},{5... | collective-permute-start | bytes 1572872 | tf_op jit(solution)/shard_map/ppermute | solution.py:36
  50.8 0.6 collective-permute-start.22
  51.5 1.3 %collective-permute-start.24 = (bf16[8,128,256]{2,1,0:T(8,128)(2,1)S(1)}, bf16[8,128,256]{2,1,0:T(8,128)(2,1)S(1)}, u32[]{:S(2)}, u32[]{:S(2)}) collective-permute-start(bf16[8,128,256]{2,1,0:T(8,128)(2,1)S(1)} %get-tuple-element.27.refs_0_), channel_id=1, source_target_pairs={{0,24},{4,28},{8,16},{12,20},{16,8},{20,12},{24,0},{28,4},{1,25},{... | collective-permute-start | bytes 1572872 | tf_op jit(solution)/shard_map/ppermute | solution.py:36
  52.7 1.3 %gram.1 = f32[264,128]{1,0:T(8,128)S(1)} custom-call(f32[16,64,256]{2,1,0:T(8,128)S(1)} %get-tuple-element.26.extrap_ref.refs_2_, f32[16,64,256]{2,1,0:T(8,128)S(1)} %copy-done), custom_call_target="tpu_custom_call" | custom-call | tf_op jit(solution)/shard_map/gram/pallas_call | solution.py:257
  54.1 0.1 pad_maximum_fusion.8
  54.3 3.3 %collective-permute-start.15 = (f32[2,68,256]{2,1,0:T(8,128)S(1)}, f32[2,68,256]{2,1,0:T(8,128)S(1)}, u32[]{:S(2)}, u32[]{:S(2)}) collective-permute-start(f32[2,68,256]{2,1,0:T(8,128)S(1)} %get-tuple-element.32), channel_id=1, source_target_pairs={{1,2},{2,1},{5,6},{6,5},{9,10},{10,9},{13,14},{14,13},{17,18},{18,... | collective-permute-start | bytes 417800 | tf_op jit(solution)/shard_map/ppermute | solution.py:49
  57.6 1.5 %collective-permute-done.17 = f32[264,128]{1,0:T(8,128)S(1)} collective-permute-done((f32[264,128]{1,0:T(8,128)S(1)}, f32[264,128]{1,0:T(8,128)S(1)}, u32[]{:S(2)}, u32[]{:S(2)}) %collective-permute-start.17) | collective-permute-done | bytes 135200 | tf_op jit(solution)/shard_map/ppermute | solution.py:36
  59.8 1.6 %collective-permute-done.15 = f32[2,68,256]{2,1,0:T(8,128)S(1)} collective-permute-done((f32[2,68,256]{2,1,0:T(8,128)S(1)}, f32[2,68,256]{2,1,0:T(8,128)S(1)}, u32[]{:S(2)}, u32[]{:S(2)}) %collective-permute-start.15) | collective-permute-done | bytes 139296 | tf_op jit(solution)/shard_map/ppermute | solution.py:49
  61.3 2.9 %collective-permute-done.16 = f32[2,68,256]{2,1,0:T(8,128)S(1)} collective-permute-done((f32[2,68,256]{2,1,0:T(8,128)S(1)}, f32[2,68,256]{2,1,0:T(8,128)S(1)}, u32[]{:S(2)}, u32[]{:S(2)}) %collective-permute-start.16) | collective-permute-done | bytes 139296 | tf_op jit(solution)/shard_map/ppermute | solution.py:36
  64.2 0.6 collective-permute-start.18
  64.9 0.1 pad_maximum_fusion
  65.0 0.1 collective-permute-start.21
  65.1 10.6 %collective-permute-done.22.refs_4_ = bf16[8,128,256]{2,1,0:T(8,128)(2,1)S(1)} collective-permute-done((bf16[8,128,256]{2,1,0:T(8,128)(2,1)S(1)}, bf16[8,128,256]{2,1,0:T(8,128)(2,1)S(1)}, u32[]{:S(2)}, u32[]{:S(2)}) %collective-permute-start.22) | collective-permute-done | bytes 524320 | tf_op jit(solution)/shard_map/ppermute | solution.py:36
  75.7 0.5 collective-permute-start.25
  76.2 0.4 fusion
  76.6 1.6 %fusion.11 = f32[16,64,256]{2,1,0:T(8,128)} fusion(f32[16,64,256]{2,1,0:T(8,128)S(1)} %copy-done.3, f32[16,68,256]{2,1,0:T(8,128)S(1)} %fusion), kind=kLoop, calls=%fused_computation.26 | loop fusion | flops 2621440 | bytes 6291456 | tf_op jit(solution)/shard_map/jit(clip)/min | solution.py:572
  78.2 5.9 %rank.1 = f32[16,64,256]{2,1,0:T(8,128)} custom-call(s32[1]{0:T(128)S(6)} %copy.14.keep_ref, f32[264,128]{1,0:T(8,128)S(1)} %add.101.refs_0_, f32[264,128]{1,0:T(8,128)S(1)} %collective-permute-done.18.refs_1_, f32[16,64,256]{2,1,0:T(8,128)S(1)} %get-tuple-element.26.extrap_ref.refs_2_, f32[16,64,256]{2,1,0:T(8,128)S(1)} %copy-done), custom_call_target="tpu_custom_call" | custom-call | tf_op jit(solution)/shard_map/rank/pallas_call | solution.py:350
  84.1 8.4 %forward.1 = f32[1,2,1024,256]{3,2,1,0:T(8,128)} custom-call(s32[8,2,24]{2,1,0:T(2,128)} %tiles_hbm.1, s32[2,8]{1,0:T(2,128)} %bitcast.38, bf16[1,2,24,1024,128]{4,3,2,1,0:T(8,128)(2,1)} %degrid_hbm.3, f32[1,2,1024,256]{3,2,1,0:T(8,128)} %dual_hbm.3, bf16[1,2,1024,256]{3,2,1,0:T(8,128)(2,1)} %seen_hbm.1, f32[1,2,256]{2,1,0:T(2,128)S(1)} %copy-done.2, ...), custom_call_target="tpu_custom_call" | custom-call | tf_op jit(solution)/shard_map/forward/pallas_call | solution.py:445
  (37 shorter events, 0.4 us)
Async XLA Ops:
  1.6 11.7 %collective-permute-start = (f32[16,2,256]{2,1,0:T(2,128)S(1)}, f32[16,2,256]{2,1,0:T(2,128)S(1)}, u32[]{:S(2)}, u32[]{:S(2)}) collective-permute-start(f32[16,2,256]{2,1,0:T(2,128)S(1)} %get-tuple-element.40), channel_id=1, source_target_pairs={{4,8},{12,16},{20,24},{8,4},{16,12},{24,20},{5,9},{13,17},{21,25},... | collective-permute-start | bytes 98312 | tf_op jit(solution)/shard_map/ppermute | solution.py:49
  3.6 9.8 %collective-permute-start.1 = (f32[16,2,256]{2,1,0:T(2,128)S(1)}, f32[16,2,256]{2,1,0:T(2,128)S(1)}, u32[]{:S(2)}, u32[]{:S(2)}) collective-permute-start(f32[16,2,256]{2,1,0:T(2,128)S(1)} %get-tuple-element.41), channel_id=1, source_target_pairs={{0,4},{4,0},{8,12},{12,8},{16,20},{20,16},{24,28},{28,24},{1,5},{5... | collective-permute-start | bytes 98312 | tf_op jit(solution)/shard_map/ppermute | solution.py:36
  5.2 8.2 %copy-start.3 = (f32[16,64,256]{2,1,0:T(8,128)S(1)}, f32[16,64,256]{2,1,0:T(8,128)}, u32[]{:S(2)}) copy-start(f32[16,64,256]{2,1,0:T(8,128)} %param.11) | copy-start | bytes 3145732
  13.3 8.7 %collective-permute-start.7 = (bf16[8,256,128]{2,1,0:T(8,128)(2,1)S(1)}, bf16[8,256,128]{2,1,0:T(8,128)(2,1)S(1)}, u32[]{:S(2)}, u32[]{:S(2)}) collective-permute-start(bf16[8,256,128]{2,1,0:T(8,128)(2,1)S(1)} %get-tuple-element.24), channel_id=1, source_target_pairs={{0,4},{4,0},{8,12},{12,8},{16,20},{20,16},{24,28},{28,24},{1,5},{5... | collective-permute-start | bytes 1572872 | tf_op jit(solution)/shard_map/ppermute | solution.py:36
  13.6 6.3 %collective-permute-start.2 = (f32[2,68,256]{2,1,0:T(8,128)S(1)}, f32[2,68,256]{2,1,0:T(8,128)S(1)}, u32[]{:S(2)}, u32[]{:S(2)}) collective-permute-start(f32[2,68,256]{2,1,0:T(8,128)S(1)} %get-tuple-element.34), channel_id=1, source_target_pairs={{0,1},{1,0},{2,3},{3,2},{4,5},{5,4},{6,7},{7,6},{8,9},{9,8},{10,11... | collective-permute-start | bytes 417800 | tf_op jit(solution)/shard_map/ppermute | solution.py:36
  14.1 7.7 %collective-permute-start.3 = (f32[2,68,256]{2,1,0:T(8,128)S(1)}, f32[2,68,256]{2,1,0:T(8,128)S(1)}, u32[]{:S(2)}, u32[]{:S(2)}) collective-permute-start(f32[2,68,256]{2,1,0:T(8,128)S(1)} %get-tuple-element.35), channel_id=1, source_target_pairs={{1,2},{2,1},{5,6},{6,5},{9,10},{10,9},{13,14},{14,13},{17,18},{18,... | collective-permute-start | bytes 417800 | tf_op jit(solution)/shard_map/ppermute | solution.py:49
  17.2 14.0 %collective-permute-start.5 = (bf16[2,8,256,128]{3,2,1,0:T(8,128)(2,1)S(1)}, bf16[2,8,256,128]{3,2,1,0:T(8,128)(2,1)S(1)}, u32[]{:S(2)}, u32[]{:S(2)}) collective-permute-start(bf16[2,8,256,128]{3,2,1,0:T(8,128)(2,1)S(1)} %get-tuple-element.22), channel_id=1, source_target_pairs={{0,4},{4,0},{8,12},{12,8},{16,20},{20,16},{24,28},{28,24},{1,5},{5... | collective-permute-start | bytes 3145736 | tf_op jit(solution)/shard_map/ppermute | solution.py:36
  17.3 18.9 %collective-permute-start.4 = (bf16[8,256,128]{2,1,0:T(8,128)(2,1)S(1)}, bf16[8,256,128]{2,1,0:T(8,128)(2,1)S(1)}, u32[]{:S(2)}, u32[]{:S(2)}) collective-permute-start(bf16[8,256,128]{2,1,0:T(8,128)(2,1)S(1)} %get-tuple-element.20), channel_id=1, source_target_pairs={{0,4},{4,0},{8,12},{12,8},{16,20},{20,16},{24,28},{28,24},{1,5},{5... | collective-permute-start | bytes 1572872 | tf_op jit(solution)/shard_map/ppermute | solution.py:36
  22.1 7.5 %collective-permute-start.10 = (bf16[4,256,128]{2,1,0:T(8,128)(2,1)S(1)}, bf16[4,256,128]{2,1,0:T(8,128)(2,1)S(1)}, u32[]{:S(2)}, u32[]{:S(2)}) collective-permute-start(bf16[4,256,128]{2,1,0:T(8,128)(2,1)S(1)} %get-tuple-element.38), channel_id=1, source_target_pairs={{0,16},{4,20},{8,24},{12,28},{16,0},{20,4},{24,8},{28,12},{1,17},{... | collective-permute-start | bytes 786440 | tf_op jit(solution)/shard_map/ppermute | solution.py:36
  22.5 8.7 %collective-permute-start.8 = (bf16[4,256,128]{2,1,0:T(8,128)(2,1)S(1)}, bf16[4,256,128]{2,1,0:T(8,128)(2,1)S(1)}, u32[]{:S(2)}, u32[]{:S(2)}) collective-permute-start(bf16[4,256,128]{2,1,0:T(8,128)(2,1)S(1)} %get-tuple-element.39), channel_id=1, source_target_pairs={{0,8},{4,12},{8,0},{12,4},{16,24},{20,28},{24,16},{28,20},{1,9},{5... | collective-permute-start | bytes 786440 | tf_op jit(solution)/shard_map/ppermute | solution.py:36
  31.4 4.3 %copy-start = (f32[16,64,256]{2,1,0:T(8,128)S(1)}, f32[16,64,256]{2,1,0:T(8,128)}, u32[]{:S(2)}) copy-start(f32[16,64,256]{2,1,0:T(8,128)} %refs_3_.1) | copy-start | bytes 3145732
  31.4 9.2 %collective-permute-start.11 = (bf16[4,256,128]{2,1,0:T(8,128)(2,1)S(1)}, bf16[4,256,128]{2,1,0:T(8,128)(2,1)S(1)}, u32[]{:S(2)}, u32[]{:S(2)}) collective-permute-start(bf16[4,256,128]{2,1,0:T(8,128)(2,1)S(1)} %get-tuple-element.30), channel_id=1, source_target_pairs={{0,8},{4,12},{8,0},{12,4},{16,24},{20,28},{24,16},{28,20},{1,9},{5... | collective-permute-start | bytes 786440 | tf_op jit(solution)/shard_map/ppermute | solution.py:36
  33.2 9.2 %collective-permute-start.9 = (bf16[4,256,128]{2,1,0:T(8,128)(2,1)S(1)}, bf16[4,256,128]{2,1,0:T(8,128)(2,1)S(1)}, u32[]{:S(2)}, u32[]{:S(2)}) collective-permute-start(bf16[4,256,128]{2,1,0:T(8,128)(2,1)S(1)} %get-tuple-element.31), channel_id=1, source_target_pairs={{0,16},{4,20},{8,24},{12,28},{16,0},{20,4},{24,8},{28,12},{1,17},{... | collective-permute-start | bytes 786440 | tf_op jit(solution)/shard_map/ppermute | solution.py:36
  33.7 11.5 %collective-permute-start.12 = (bf16[4,256,128]{2,1,0:T(8,128)(2,1)S(1)}, bf16[4,256,128]{2,1,0:T(8,128)(2,1)S(1)}, u32[]{:S(2)}, u32[]{:S(2)}) collective-permute-start(bf16[4,256,128]{2,1,0:T(8,128)(2,1)S(1)} %get-tuple-element.28), channel_id=1, source_target_pairs={{0,16},{4,20},{8,24},{12,28},{16,0},{20,4},{24,8},{28,12},{1,17},{... | collective-permute-start | bytes 786440 | tf_op jit(solution)/shard_map/ppermute | solution.py:36
  35.4 9.8 %copy-start.1 = (f32[16,64,256]{2,1,0:T(8,128)S(1)}, f32[16,64,256]{2,1,0:T(8,128)}, u32[]{:S(2)}) copy-start(f32[16,64,256]{2,1,0:T(8,128)} %refs_0_.1) | copy-start | bytes 3145732
  35.4 9.8 %collective-permute-start.6 = (bf16[4,256,128]{2,1,0:T(8,128)(2,1)S(1)}, bf16[4,256,128]{2,1,0:T(8,128)(2,1)S(1)}, u32[]{:S(2)}, u32[]{:S(2)}) collective-permute-start(bf16[4,256,128]{2,1,0:T(8,128)(2,1)S(1)} %get-tuple-element.29), channel_id=1, source_target_pairs={{0,8},{4,12},{8,0},{12,4},{16,24},{20,28},{24,16},{28,20},{1,9},{5... | collective-permute-start | bytes 786440 | tf_op jit(solution)/shard_map/ppermute | solution.py:36
  46.7 7.3 %collective-permute-start.13 = (f32[16,2,256]{2,1,0:T(2,128)S(1)}, f32[16,2,256]{2,1,0:T(2,128)S(1)}, u32[]{:S(2)}, u32[]{:S(2)}) collective-permute-start(f32[16,2,256]{2,1,0:T(2,128)S(1)} %get-tuple-element.36), channel_id=1, source_target_pairs={{4,8},{12,16},{20,24},{8,4},{16,12},{24,20},{5,9},{13,17},{21,25},... | collective-permute-start | bytes 98312 | tf_op jit(solution)/shard_map/ppermute | solution.py:49
  48.6 5.4 %collective-permute-start.14 = (f32[16,2,256]{2,1,0:T(2,128)S(1)}, f32[16,2,256]{2,1,0:T(2,128)S(1)}, u32[]{:S(2)}, u32[]{:S(2)}) collective-permute-start(f32[16,2,256]{2,1,0:T(2,128)S(1)} %get-tuple-element.37), channel_id=1, source_target_pairs={{0,4},{4,0},{8,12},{12,8},{16,20},{20,16},{24,28},{28,24},{1,5},{5... | collective-permute-start | bytes 98312 | tf_op jit(solution)/shard_map/ppermute | solution.py:36
  49.2 15.8 %collective-permute-start.20 = (bf16[8,128,256]{2,1,0:T(8,128)(2,1)S(1)}, bf16[8,128,256]{2,1,0:T(8,128)(2,1)S(1)}, u32[]{:S(2)}, u32[]{:S(2)}) collective-permute-start(bf16[8,128,256]{2,1,0:T(8,128)(2,1)S(1)} %get-tuple-element.27.refs_0_), channel_id=1, source_target_pairs={{0,8},{4,12},{8,0},{12,4},{16,24},{20,28},{24,16},{28,20},{1,9},{5... | collective-permute-start | bytes 1572872 | tf_op jit(solution)/shard_map/ppermute | solution.py:36
  50.8 24.9 %collective-permute-start.22 = (bf16[8,128,256]{2,1,0:T(8,128)(2,1)S(1)}, bf16[8,128,256]{2,1,0:T(8,128)(2,1)S(1)}, u32[]{:S(2)}, u32[]{:S(2)}) collective-permute-start(bf16[8,128,256]{2,1,0:T(8,128)(2,1)S(1)} %get-tuple-element.27.refs_0_), channel_id=1, source_target_pairs={{0,16},{4,20},{8,24},{12,28},{16,0},{20,4},{24,8},{28,12},{1,17},{... | collective-permute-start | bytes 1572872 | tf_op jit(solution)/shard_map/ppermute | solution.py:36
  51.5 24.2 %collective-permute-start.24 = (bf16[8,128,256]{2,1,0:T(8,128)(2,1)S(1)}, bf16[8,128,256]{2,1,0:T(8,128)(2,1)S(1)}, u32[]{:S(2)}, u32[]{:S(2)}) collective-permute-start(bf16[8,128,256]{2,1,0:T(8,128)(2,1)S(1)} %get-tuple-element.27.refs_0_), channel_id=1, source_target_pairs={{0,24},{4,28},{8,16},{12,20},{16,8},{20,12},{24,0},{28,4},{1,25},{... | collective-permute-start | bytes 1572872 | tf_op jit(solution)/shard_map/ppermute | solution.py:36
  54.0 5.1 %collective-permute-start.17 = (f32[264,128]{1,0:T(8,128)S(1)}, f32[264,128]{1,0:T(8,128)S(1)}, u32[]{:S(2)}, u32[]{:S(2)}) collective-permute-start(f32[264,128]{1,0:T(8,128)S(1)} %gram.1), channel_id=1, source_target_pairs={{0,1},{1,0},{2,3},{3,2},{4,5},{5,4},{6,7},{7,6},{8,9},{9,8},{10,11... | collective-permute-start | bytes 405512 | tf_op jit(solution)/shard_map/ppermute | solution.py:36
  54.3 7.0 %collective-permute-start.15 = (f32[2,68,256]{2,1,0:T(8,128)S(1)}, f32[2,68,256]{2,1,0:T(8,128)S(1)}, u32[]{:S(2)}, u32[]{:S(2)}) collective-permute-start(f32[2,68,256]{2,1,0:T(8,128)S(1)} %get-tuple-element.32), channel_id=1, source_target_pairs={{1,2},{2,1},{5,6},{6,5},{9,10},{10,9},{13,14},{14,13},{17,18},{18,... | collective-permute-start | bytes 417800 | tf_op jit(solution)/shard_map/ppermute | solution.py:49
  59.1 5.1 %collective-permute-start.16 = (f32[2,68,256]{2,1,0:T(8,128)S(1)}, f32[2,68,256]{2,1,0:T(8,128)S(1)}, u32[]{:S(2)}, u32[]{:S(2)}) collective-permute-start(f32[2,68,256]{2,1,0:T(8,128)S(1)} %get-tuple-element.33), channel_id=1, source_target_pairs={{0,1},{1,0},{2,3},{3,2},{4,5},{5,4},{6,7},{7,6},{8,9},{9,8},{10,11... | collective-permute-start | bytes 417800 | tf_op jit(solution)/shard_map/ppermute | solution.py:36
  61.3 22.7 %collective-permute-start.19 = (bf16[8,128,256]{2,1,0:T(8,128)(2,1)S(1)}, bf16[8,128,256]{2,1,0:T(8,128)(2,1)S(1)}, u32[]{:S(2)}, u32[]{:S(2)}) collective-permute-start(bf16[8,128,256]{2,1,0:T(8,128)(2,1)S(1)} %get-tuple-element.27.refs_0_), channel_id=1, source_target_pairs={{0,4},{4,0},{8,12},{12,8},{16,20},{20,16},{24,28},{28,24},{1,5},{5... | collective-permute-start | bytes 1572872 | tf_op jit(solution)/shard_map/ppermute | solution.py:36
  64.2 14.0 %collective-permute-start.18 = (f32[264,128]{1,0:T(8,128)S(1)}, f32[264,128]{1,0:T(8,128)S(1)}, u32[]{:S(2)}, u32[]{:S(2)}) collective-permute-start(f32[264,128]{1,0:T(8,128)S(1)} %add.101.refs_0_), channel_id=1, source_target_pairs={{0,2},{1,3},{2,0},{3,1},{4,6},{5,7},{6,4},{7,5},{8,10},{9,11},{10,... | collective-permute-start | bytes 405512 | tf_op jit(solution)/shard_map/ppermute | solution.py:36
  65.0 19.0 %collective-permute-start.21 = (bf16[8,128,256]{2,1,0:T(8,128)(2,1)S(1)}, bf16[8,128,256]{2,1,0:T(8,128)(2,1)S(1)}, u32[]{:S(2)}, u32[]{:S(2)}) collective-permute-start(bf16[8,128,256]{2,1,0:T(8,128)(2,1)S(1)} %collective-permute-done.20.refs_2_), channel_id=1, source_target_pairs={{0,4},{4,0},{8,12},{12,8},{16,20},{20,16},{24,28},{28,24},{1,5},{5... | collective-permute-start | bytes 1572872 | tf_op jit(solution)/shard_map/ppermute | solution.py:36
  75.7 8.4 %collective-permute-start.23 = (bf16[8,128,256]{2,1,0:T(8,128)(2,1)S(1)}, bf16[8,128,256]{2,1,0:T(8,128)(2,1)S(1)}, u32[]{:S(2)}, u32[]{:S(2)}) collective-permute-start(bf16[8,128,256]{2,1,0:T(8,128)(2,1)S(1)} %collective-permute-done.22.refs_4_), channel_id=1, source_target_pairs={{0,4},{4,0},{8,12},{12,8},{16,20},{20,16},{24,28},{28,24},{1,5},{5... | collective-permute-start | bytes 1572872 | tf_op jit(solution)/shard_map/ppermute | solution.py:36
  75.7 8.4 %collective-permute-start.25 = (bf16[8,128,256]{2,1,0:T(8,128)(2,1)S(1)}, bf16[8,128,256]{2,1,0:T(8,128)(2,1)S(1)}, u32[]{:S(2)}, u32[]{:S(2)}) collective-permute-start(bf16[8,128,256]{2,1,0:T(8,128)(2,1)S(1)} %collective-permute-done.24.refs_6_), channel_id=1, source_target_pairs={{0,4},{4,0},{8,12},{12,8},{16,20},{20,16},{24,28},{28,24},{1,5},{5... | collective-permute-start | bytes 1572872 | tf_op jit(solution)/shard_map/ppermute | solution.py:36
  78.2 5.9 %copy-start.2 = (f32[1,2,256]{2,1,0:T(2,128)S(1)}, f32[1,2,256]{2,1,0:T(2,128)}, u32[]{:S(2)}) copy-start(f32[1,2,256]{2,1,0:T(2,128)} %radius_ref.1) | copy-start | bytes 6148
where the time goes:
time: 92.9 us; the launch traced here: 92.7 us
  waiting for transfers between devices  35.1 us (38%)
  starting transfers between devices  25.8 us (28%)
  Pallas kernels  25 us (27%)
  other arithmetic  5 us (5%)
  between operations  1.78 us (2%)
    ppermute x22, waiting for transfers between devices, swap(): return lax.ppermute(value, axis, [(i, i ^ mask) for i in range(count)])  31.6 us
    ppermute x22, starting transfers between devices, swap(): return lax.ppermute(value, axis, [(i, i ^ mask) for i in range(count)])  15.6 us
    ppermute x4, starting transfers between devices, padded_2(): outside = lax.ppermute(outward, axis, outer)  10.2 us
    pallas_call x1, Pallas kernels, forward(): pl.pallas_call(functools.partial(forward_body, chips=chips, tile_count=ti...  8.43 us
    pallas_call x1, Pallas kernels, adjoint(): pl.pallas_call(functools.partial(adjoint_body, chips=chips, tile_count=ti...  8.05 us
    pallas_call x1, Pallas kernels, rank_update(): pl.pallas_call(functools.partial(rank_body, parts=len(packed)), out_shape...  5.86 us
    ppermute x4, waiting for transfers between devices, padded_2(): outside = lax.ppermute(outward, axis, outer)  3.47 us
  transfers between devices with their start and end apart: 26, of which 11 were waited for; matrix products, arithmetic and copies ran while one was open for 4% of the time, Pallas kernels for 16%

commit v1 on v0

--- a/solution.py
+++ b/solution.py
@@ -25,6 +25,7 @@
 vmem_spec = pl.BlockSpec(memory_space=pltpu.VMEM)
 adjoint_group = 8
 forward_group = 8
+forward_limit = 32
 
 
 def in_hbm(value):
@@ -122,10 +123,12 @@
     duals = [
         pltpu.make_async_copy(dual_hbm.at[0, b], dual.at[b], dual_sems.at[b]) for b in range(blocks)
     ]
-    for copy in lists + duals:
+    for copy in lists:
         copy.start()
     for b in range(blocks):
+        duals[b].start()
         chunks[b][0].start()
+    acc[...] = jnp.zeros_like(acc)
     for copy in lists:
         copy.wait()
     for b in range(blocks):
@@ -134,11 +137,9 @@
             def _():
                 chunks[b][c].start()
     live = 2 * chips * tile_count
-    acc[...] = jnp.zeros_like(acc)
     for b in range(blocks):
         duals[b].wait()
         turned[b] = dual[b].astype(jnp.bfloat16).T
-    for b in range(blocks):
         for c in range(depth // group):
             @pl.when(c * group < counts[b, me])
             def _():
@@ -197,10 +198,9 @@
 
 
 def primal_body(*refs, parts):
-    sky_ref, rest_ref, own_ref, mate_ref = refs[:4]
-    halves = (refs[4 : 4 + parts], refs[4 + parts : 4 + 2 * parts])
-    next_ref, extrap_ref = refs[4 + 2 * parts : 6 + 2 * parts]
-    tiles_ref = refs[6 + 2 * parts]
+    sky_ref, base_ref, rest_ref, own_ref, mate_ref = refs[:5]
+    halves = (refs[5 : 5 + parts], refs[5 + parts : 5 + 2 * parts])
+    next_ref, extrap_ref, tiles_ref = refs[5 + 2 * parts :]
     _, columns, channels = sky_ref.shape
     across = columns // TC
     half = tiles_ref.shape[0] // 2
@@ -214,24 +214,26 @@
             rows = pl.ds(tile // across * TR, TR)
             cols = pl.ds(tile % across * TC, TC)
             sky = sky_ref[rows, cols, :]
-            new = jnp.maximum(sky - step_primal * (back + rest_ref[rows, cols, :]), 0.0)
+            new = jnp.maximum(
+                base_ref[rows, cols, :] - step_primal * (back + rest_ref[rows, cols, :]), 0.0
+            )
             extrap = 2.0 * new - sky
             next_ref[rows, cols, :] = new
             extrap_ref[rows, cols, :] = extrap
             tiles_ref[tile] = extrap.reshape(TR * TC, channels).astype(jnp.bfloat16)
 
 
-def primal(sky, rest, own, mate, low, high):
+def primal(sky, base, rest, own, mate, low, high):
     whole = jax.ShapeDtypeStruct(sky.shape, jnp.float32)
     tiles = jax.ShapeDtypeStruct((own.shape[0], own.shape[2], own.shape[1]), jnp.bfloat16)
     return pl.pallas_call(
         functools.partial(primal_body, parts=len(low)),
         out_shape=[whole, whole, tiles],
-        in_specs=[vmem_spec] * (4 + len(low) + len(high)),
+        in_specs=[vmem_spec] * (5 + len(low) + len(high)),
         out_specs=[vmem_spec] * 3,
-        compiler_params=pltpu.CompilerParams(vmem_limit_bytes=24 * MIB),
+        compiler_params=pltpu.CompilerParams(vmem_limit_bytes=16 * MIB),
         name="primal",
-    )(sky, rest, own, mate, *low, *high)
+    )(sky, base, rest, own, mate, *low, *high)
 
 
 def gram_body(extrap_ref, rank_ref, packed_ref):
@@ -259,7 +261,7 @@
         out_shape=jax.ShapeDtypeStruct((channels + 8, channels // 2), jnp.float32),
         in_specs=[vmem_spec, vmem_spec],
         out_specs=vmem_spec,
-        compiler_params=pltpu.CompilerParams(vmem_limit_bytes=24 * MIB),
+        compiler_params=pltpu.CompilerParams(vmem_limit_bytes=16 * MIB),
         name="gram",
     )(extrap, rank_dual)
 
@@ -272,10 +274,10 @@
 def dot_fine(left, right):
     a, b = split(left)
     c, d = split(right)
-    return (
-        jnp.dot(a, c, preferred_element_type=jnp.float32)
-        + jnp.dot(a, d, preferred_element_type=jnp.float32)
-        + jnp.dot(b, c, preferred_element_type=jnp.float32)
+    return jnp.dot(
+        jnp.concatenate([a, a, b], axis=1),
+        jnp.concatenate([c, d, c], axis=0),
+        preferred_element_type=jnp.float32,
     )
 
 
@@ -335,9 +337,9 @@
             error = both[channels:]
         else:
             inverse = inverse + dot_quick(inverse, error)
-    for _ in range(2):
-        residual = eye - dot_fine(system, inverse)
-        inverse = inverse + dot_fine(inverse, residual)
+    residual = eye - dot_fine(system, inverse)
+    residual = residual + dot_quick(residual, residual)
+    inverse = inverse + dot_fine(inverse, residual)
     residual = eye - dot_full(system, inverse)
     inverse = inverse + dot_fine(inverse, residual)
     for load in loads:
@@ -357,58 +359,35 @@
             pltpu.VMEM(extrap.shape, jnp.float32),
             pltpu.SemaphoreType.DMA((2,)),
         ],
-        compiler_params=pltpu.CompilerParams(vmem_limit_bytes=32 * MIB),
+        compiler_params=pltpu.CompilerParams(vmem_limit_bytes=12 * MIB),
         name="rank",
     )(keep_count, *packed, extrap, rank_dual)
 
 
 def forward_body(
-    tiles_hbm, counts_hbm, degrid_hbm, dual_hbm, seen_hbm, radius_ref, *refs,
-    chips, tile_count, group,
+    tiles, counts, degrid_ref, dual_hbm, seen_hbm, radius_ref, *refs, chips, tile_count, group
 ):
-    held = 2 * chips
-    image_refs, out_hbm = refs[:held], refs[held]
-    tiles, counts, dual, seen, image, acc, buf, sems, image_sems, wide_sems, list_sems = refs[
-        held + 1 :
+    image_refs, out_hbm = refs[:-8], refs[-8]
+    image, acc, dual, seen, image_sems, load_sems, store_sems = refs[-7:]
+    blocks, depth, _, _ = degrid_ref.shape[1:5]
+    me = lax.axis_index("facet")
+    images = []
+    live = 0
+    for i, ref in enumerate(image_refs):
+        size = ref.shape[0]
+        images.append(
+            pltpu.make_async_copy(ref, image.at[pl.ds(live, size)], image_sems.at[i])
+        )
+        live += size
+    stores = [
+        pltpu.make_async_copy(acc.at[b], out_hbm.at[0, b], store_sems.at[b]) for b in range(blocks)
     ]
-    blocks, depth, _, _ = degrid_hbm.shape[1:5]
-    me = lax.axis_index("facet")
-    chunks = slot_chunks(degrid_hbm, buf, sems, group)
-    lists = [
-        pltpu.make_async_copy(counts_hbm, counts, list_sems.at[0]),
-        pltpu.make_async_copy(tiles_hbm, tiles, list_sems.at[1]),
+    loads = [
+        pltpu.make_async_copy(dual_hbm.at[0], dual, load_sems.at[0]),
+        pltpu.make_async_copy(seen_hbm.at[0], seen, load_sems.at[1]),
     ]
-    images = [
-        pltpu.make_async_copy(
-            image_refs[i], image.at[pl.ds(i * tile_count, tile_count)], image_sems.at[i]
-        )
-        for i in range(held)
-    ]
-    wide = [
-        pltpu.make_async_copy(dual_hbm.at[0], dual, wide_sems.at[0]),
-        pltpu.make_async_copy(seen_hbm.at[0], seen, wide_sems.at[1]),
-    ]
-    stores = [
-        pltpu.make_async_copy(acc.at[b], out_hbm.at[0, b], wide_sems.at[2 + b]) for b in range(blocks)
-    ]
-    for copy in lists:
+    for copy in images + loads:
         copy.start()
-    chunks[0][0].start()
-    for copy in images:
-        copy.start()
-    for b in range(1, blocks):
-        chunks[b][0].start()
-    for copy in lists:
-        copy.wait()
-    for b in range(blocks):
-        for c in range(1, depth // group):
-            @pl.when(c * group < counts[b, me])
-            def _():
-                chunks[b][c].start()
-        if b == 0:
-            for copy in wide:
-                copy.start()
-    live = held * tile_count
     image[live] = jnp.zeros_like(image[live])
     for copy in images:
         copy.wait()
@@ -416,18 +395,19 @@
         for c in range(depth // group):
             @pl.when(c * group < counts[b, me])
             def _():
-                chunks[b][c].wait()
                 names = [
                     relative_tile(tiles, me, b, c * group + j, counts[b, me], tile_count, live)
                     for j in range(group)
                 ]
-                left = jnp.concatenate([buf[b, c * group + j] for j in range(group)], axis=1)
+                left = jnp.concatenate(
+                    [degrid_ref[0, b, c * group + j] for j in range(group)], axis=1
+                )
                 right = jnp.concatenate([image[name] for name in names], axis=0)
                 product = jnp.dot(left, right, preferred_element_type=jnp.float32)
                 acc[b] = acc[b] + product if c else product
 
         if b == 0:
-            for copy in wide:
+            for copy in loads:
                 copy.wait()
         misfit = acc[b] + (dual[b] - seen[b].astype(jnp.float32))
         size = jnp.sqrt(jnp.sum(misfit * misfit, axis=0, keepdims=True) + 1e-06)
@@ -439,34 +419,27 @@
 
 
 def forward(tile_list, counts, degrid, dual, observed, radius, image, chips, tile_count):
-    _, blocks, depth, entries, pixels = degrid.shape
+    _, blocks, _, entries, pixels = degrid.shape
     channels = dual.shape[-1]
     group = forward_group
     return pl.pallas_call(
         functools.partial(forward_body, chips=chips, tile_count=tile_count, group=group),
         out_shape=jax.ShapeDtypeStruct(dual.shape, jnp.float32),
-        in_specs=[hbm_spec] * 5 + [vmem_spec] + [any_spec] * len(image),
+        in_specs=[smem_spec, smem_spec, vmem_spec, hbm_spec, hbm_spec, vmem_spec]
+        + [any_spec] * len(image),
         out_specs=hbm_spec,
         scratch_shapes=[
-            pltpu.SMEM(tile_list.shape, jnp.int32),
-            pltpu.SMEM(counts.shape, jnp.int32),
+            pltpu.VMEM((2 * chips * tile_count + 1, pixels, channels), jnp.bfloat16),
+            pltpu.VMEM((blocks, entries, channels), jnp.float32),
             pltpu.VMEM((blocks, entries, channels), jnp.float32),
             pltpu.VMEM((blocks, entries, channels), jnp.bfloat16),
-            pltpu.VMEM((2 * chips * tile_count + 1, pixels, channels), jnp.bfloat16),
-            pltpu.VMEM((blocks, entries, channels), jnp.float32),
-            pltpu.VMEM((blocks, depth, entries, pixels), jnp.bfloat16),
-            pltpu.SemaphoreType.DMA((blocks, depth // group)),
-            pltpu.SemaphoreType.DMA((2 * chips,)),
-            pltpu.SemaphoreType.DMA((2 + blocks,)),
+            pltpu.SemaphoreType.DMA((len(image),)),
             pltpu.SemaphoreType.DMA((2,)),
+            pltpu.SemaphoreType.DMA((blocks,)),
         ],
-        compiler_params=pltpu.CompilerParams(vmem_limit_bytes=32 * MIB),
+        compiler_params=pltpu.CompilerParams(vmem_limit_bytes=forward_limit * MIB),
         name="forward",
-    )(
-        *(in_hbm(value) for value in (tile_list, counts, degrid, dual, observed)),
-        radius,
-        *image,
-    )
+    )(tile_list, counts, degrid, in_hbm(dual), in_hbm(observed), radius, *image)
 
 
 def plus(*values):
@@ -502,13 +475,19 @@
 
 
 def from_owners(tiles, chips):
-    reached = [tiles]
-    for k in range(1, chips):
-        reached.append(swap(tiles, "facet", 2 * k))
+    reached = [[tiles]]
+    if chips == 4:
+        half = tiles.shape[0] // 2
+        x, y = swap(tiles, "facet", 2), swap(tiles, "facet", 4)
+        low = swap(x[:half], "facet", 4)
+        high = swap(y[half:], "facet", 2)
+        reached += [[x], [y], [low, high]]
+    else:
+        reached += [[swap(tiles, "facet", 2 * k)] for k in range(1, chips)]
     image = []
-    for k in range(chips):
-        image.append(reached[k])
-        image.append(swap(reached[k], "facet", 1))
+    for parts in reached:
+        image += parts
+        image += [swap(part, "facet", 1) for part in parts]
     return image
 
 
@@ -563,8 +542,9 @@
     mate_own, low, high = to_owners(sums[:3], sums[3:], chips)
 
     wave_halo = padded_2(wave_dual, sides, 2)
-    rest = synthesis(wave_halo, height, columns) + rank_dual
-    sky_next, extrap, tiles = primal(sky_image, rest, sums[2], mate_own, low, high)
+    base = sky_image - step_primal * rank_dual
+    rest = synthesis(wave_halo, height, columns)
+    sky_next, extrap, tiles = primal(sky_image, base, rest, sums[2], mate_own, low, high)
 
     image = from_owners(tiles, chips)
     packed = gram_of(extrap, rank_dual)

time: 92.9 us -> 91.2 us (0.982)
  the two profiles are of different devices: /device:TPU:10 before, /device:TPU:0 now
where the time goes in v1:
time: 91.2 us; the launch traced here: 91 us
  starting transfers between devices  33.5 us (37%)
  waiting for transfers between devices  30.1 us (33%)
  Pallas kernels  20.6 us (23%)
  other arithmetic  4.99 us (5%)
  between operations  1.82 us (2%)
    ppermute x24, starting transfers between devices, swap(): return lax.ppermute(value, axis, [(i, i ^ mask) for i in range(count)])  30.5 us
    ppermute x24, waiting for transfers between devices, swap(): return lax.ppermute(value, axis, [(i, i ^ mask) for i in range(count)])  30.1 us
    pallas_call x1, Pallas kernels, forward(): pl.pallas_call(functools.partial(forward_body, chips=chips, tile_count=ti...  6.72 us
    pallas_call x1, Pallas kernels, adjoint(): pl.pallas_call(functools.partial(adjoint_body, chips=chips, tile_count=ti...  5.77 us
    pallas_call x1, Pallas kernels, rank_update(): pl.pallas_call(functools.partial(rank_body, parts=len(packed)), out_shape...  5.39 us
    ppermute x4, starting transfers between devices, padded_2(): outside = lax.ppermute(outward, axis, outer)  2.97 us
  transfers between devices with their start and end apart: 28, of which 10 were waited for; matrix products, arithmetic and copies ran while one was open for 4% of the time, Pallas kernels for 14%

profile of v1, /device:TPU:0, one launch (start us, length us, event | category | flops | bytes accessed | tf_op | source)
XLA Modules:
  0.0 91.0 jit_solution(9310445902912276833)
XLA Ops:
  0.6 1.0 %broadcast_select_fusion.11 = (f32[16,2,256]{2,1,0:T(2,128)S(1)}, f32[16,2,256]{2,1,0:T(2,128)S(1)}) fusion(pred[]{:T(512)S(6)} %eq.6, f32[16,64,256]{2,1,0:T(8,128)} %param.11), kind=kLoop, calls=%fused_computation.65 | loop fusion | flops 16384 | bytes 131073 | tf_op jit(solution)/shard_map/jit(_where)/select_n | solution.py:48
  1.6 0.7 collective-permute-start
  2.3 4.4 %collective-permute-start.1 = (f32[16,2,256]{2,1,0:T(2,128)S(1)}, f32[16,2,256]{2,1,0:T(2,128)S(1)}, u32[]{:S(2)}, u32[]{:S(2)}) collective-permute-start(f32[16,2,256]{2,1,0:T(2,128)S(1)} %get-tuple-element.41), channel_id=1, source_target_pairs={{0,4},{4,0},{8,12},{12,8},{16,20},{20,16},{24,28},{28,24},{1,5},{5... | collective-permute-start | bytes 98312 | tf_op jit(solution)/shard_map/ppermute | solution.py:37
  6.7 5.8 %adjoint.1 = (bf16[8,256,128]{2,1,0:T(8,128)(2,1)S(1)}, bf16[2,8,256,128]{3,2,1,0:T(8,128)(2,1)S(1)}, bf16[8,256,128]{2,1,0:T(8,128)(2,1)S(1)}, bf16[8,256,128]{...) custom-call(s32[8,2,24]{2,1,0:T(2,128)} %tiles, s32[2,8]{1,0:T(2,128)} %bitcast.23, ...), custom_call_target="tpu_custom_call" | custom-call | tf_op jit(solution)/shard_map/adjoint/pallas_call | solution.py:179
  12.5 1.1 %collective-permute-start.7 = (bf16[8,256,128]{2,1,0:T(8,128)(2,1)S(1)}, bf16[8,256,128]{2,1,0:T(8,128)(2,1)S(1)}, u32[]{:S(2)}, u32[]{:S(2)}) collective-permute-start(bf16[8,256,128]{2,1,0:T(8,128)(2,1)S(1)} %get-tuple-element.24), channel_id=1, source_target_pairs={{0,4},{4,0},{8,12},{12,8},{16,20},{20,16},{24,28},{28,24},{1,5},{5... | collective-permute-start | bytes 1572872 | tf_op jit(solution)/shard_map/ppermute | solution.py:37
  13.6 0.1 pad_maximum_fusion.7
  13.8 3.2 %collective-permute-start.2 = (f32[2,68,256]{2,1,0:T(8,128)S(1)}, f32[2,68,256]{2,1,0:T(8,128)S(1)}, u32[]{:S(2)}, u32[]{:S(2)}) collective-permute-start(f32[2,68,256]{2,1,0:T(8,128)S(1)} %get-tuple-element.34), channel_id=1, source_target_pairs={{0,1},{1,0},{2,3},{3,2},{4,5},{5,4},{6,7},{7,6},{8,9},{9,8},{10,11... | collective-permute-start | bytes 417800 | tf_op jit(solution)/shard_map/ppermute | solution.py:37
  16.9 0.7 collective-permute-start.3
  17.6 0.3 collective-permute-start.5
  17.8 0.3 collective-permute-start.4
  18.2 3.2 %collective-permute-done.2 = f32[2,68,256]{2,1,0:T(8,128)S(1)} collective-permute-done((f32[2,68,256]{2,1,0:T(8,128)S(1)}, f32[2,68,256]{2,1,0:T(8,128)S(1)}, u32[]{:S(2)}, u32[]{:S(2)}) %collective-permute-start.2) | collective-permute-done | bytes 139296 | tf_op jit(solution)/shard_map/ppermute | solution.py:37
  21.4 0.1 maximum_maximum_fusion
  21.6 0.1 add_convert_fusion.1
  21.7 1.7 %collective-permute-start.10 = (bf16[4,256,128]{2,1,0:T(8,128)(2,1)S(1)}, bf16[4,256,128]{2,1,0:T(8,128)(2,1)S(1)}, u32[]{:S(2)}, u32[]{:S(2)}) collective-permute-start(bf16[4,256,128]{2,1,0:T(8,128)(2,1)S(1)} %get-tuple-element.38), channel_id=1, source_target_pairs={{0,16},{4,20},{8,24},{12,28},{16,0},{20,4},{24,8},{28,12},{1,17},{... | collective-permute-start | bytes 786440 | tf_op jit(solution)/shard_map/ppermute | solution.py:37
  23.5 0.4 fusion.4
  23.9 6.0 %collective-permute-done.10 = bf16[4,256,128]{2,1,0:T(8,128)(2,1)S(1)} collective-permute-done((bf16[4,256,128]{2,1,0:T(8,128)(2,1)S(1)}, bf16[4,256,128]{2,1,0:T(8,128)(2,1)S(1)}, u32[]{:S(2)}, u32[]{:S(2)}) %collective-permute-start.10) | collective-permute-done | bytes 262176 | tf_op jit(solution)/shard_map/ppermute | solution.py:37
  29.9 1.1 %collective-permute-done.8 = bf16[4,256,128]{2,1,0:T(8,128)(2,1)S(1)} collective-permute-done((bf16[4,256,128]{2,1,0:T(8,128)(2,1)S(1)}, bf16[4,256,128]{2,1,0:T(8,128)(2,1)S(1)}, u32[]{:S(2)}, u32[]{:S(2)}) %collective-permute-start.8) | collective-permute-done | bytes 262176 | tf_op jit(solution)/shard_map/ppermute | solution.py:37
  31.0 0.2 fusion.17
  31.3 0.3 collective-permute-start.11
  31.6 1.4 %collective-permute-start.9 = (bf16[4,256,128]{2,1,0:T(8,128)(2,1)S(1)}, bf16[4,256,128]{2,1,0:T(8,128)(2,1)S(1)}, u32[]{:S(2)}, u32[]{:S(2)}) collective-permute-start(bf16[4,256,128]{2,1,0:T(8,128)(2,1)S(1)} %get-tuple-element.31), channel_id=1, source_target_pairs={{0,16},{4,20},{8,24},{12,28},{16,0},{20,4},{24,8},{28,12},{1,17},{... | collective-permute-start | bytes 786440 | tf_op jit(solution)/shard_map/ppermute | solution.py:37
  33.0 0.1 fusion.20
  33.1 0.7 collective-permute-start.12
  33.8 1.7 %collective-permute-start.6 = (bf16[4,256,128]{2,1,0:T(8,128)(2,1)S(1)}, bf16[4,256,128]{2,1,0:T(8,128)(2,1)S(1)}, u32[]{:S(2)}, u32[]{:S(2)}) collective-permute-start(bf16[4,256,128]{2,1,0:T(8,128)(2,1)S(1)} %get-tuple-element.29), channel_id=1, source_target_pairs={{0,8},{4,12},{8,0},{12,4},{16,24},{20,28},{24,16},{28,20},{1,9},{5... | collective-permute-start | bytes 786440 | tf_op jit(solution)/shard_map/ppermute | solution.py:37
  35.6 0.5 fusion.14
  36.1 4.4 %collective-permute-done.11.refs_7_ = bf16[4,256,128]{2,1,0:T(8,128)(2,1)S(1)} collective-permute-done((bf16[4,256,128]{2,1,0:T(8,128)(2,1)S(1)}, bf16[4,256,128]{2,1,0:T(8,128)(2,1)S(1)}, u32[]{:S(2)}, u32[]{:S(2)}) %collective-permute-start.11) | collective-permute-done | bytes 262176 | tf_op jit(solution)/shard_map/ppermute | solution.py:37
  40.5 0.3 collective-permute-done.9.refs_6_
  40.8 3.1 %collective-permute-done.12.refs_8_ = bf16[4,256,128]{2,1,0:T(8,128)(2,1)S(1)} collective-permute-done((bf16[4,256,128]{2,1,0:T(8,128)(2,1)S(1)}, bf16[4,256,128]{2,1,0:T(8,128)(2,1)S(1)}, u32[]{:S(2)}, u32[]{:S(2)}) %collective-permute-start.12) | collective-permute-done | bytes 262176 | tf_op jit(solution)/shard_map/ppermute | solution.py:37
  43.9 1.4 %primal.1 = (f32[16,64,256]{2,1,0:T(8,128)}, f32[16,64,256]{2,1,0:T(8,128)S(1)}, bf16[8,128,256]{2,1,0:T(8,128)(2,1)S(1)}) custom-call(f32[16,64,256]{2,1,0:T(8,128)S(1)} %copy-done.1, f32[16,64,256]{2,1,0:T(8,128)S(1)} %get-tuple-element.51.refs_1_, f32[16,64,256]{2,1,0:T(8,128)S(1)} %get-tuple-element.50.refs_2_, ...), custom_call_target="tpu_custom_call" | custom-call | tf_op jit(solution)/shard_map/primal/pallas_call | solution.py:229
  45.4 0.7 collective-permute-start.13
  46.1 2.9 %collective-permute-start.14 = (f32[16,2,256]{2,1,0:T(2,128)S(1)}, f32[16,2,256]{2,1,0:T(2,128)S(1)}, u32[]{:S(2)}, u32[]{:S(2)}) collective-permute-start(f32[16,2,256]{2,1,0:T(2,128)S(1)} %get-tuple-element.37), channel_id=1, source_target_pairs={{0,4},{4,0},{8,12},{12,8},{16,20},{20,16},{24,28},{28,24},{1,5},{5... | collective-permute-start | bytes 98312 | tf_op jit(solution)/shard_map/ppermute | solution.py:37
  49.0 1.0 %collective-permute-start.20 = (bf16[8,128,256]{2,1,0:T(8,128)(2,1)S(1)}, bf16[8,128,256]{2,1,0:T(8,128)(2,1)S(1)}, u32[]{:S(2)}, u32[]{:S(2)}) collective-permute-start(bf16[8,128,256]{2,1,0:T(8,128)(2,1)S(1)} %get-tuple-element.27.refs_0_), channel_id=1, source_target_pairs={{0,8},{4,12},{8,0},{12,4},{16,24},{20,28},{24,16},{28,20},{1,9},{5... | collective-permute-start | bytes 1572872 | tf_op jit(solution)/shard_map/ppermute | solution.py:37
  50.0 0.1 pad_maximum_fusion.8
  50.1 1.0 %collective-permute-start.15 = (f32[2,68,256]{2,1,0:T(8,128)S(1)}, f32[2,68,256]{2,1,0:T(8,128)S(1)}, u32[]{:S(2)}, u32[]{:S(2)}) collective-permute-start(f32[2,68,256]{2,1,0:T(8,128)S(1)} %get-tuple-element.32), channel_id=1, source_target_pairs={{1,2},{2,1},{5,6},{6,5},{9,10},{10,9},{13,14},{14,13},{17,18},{18,... | collective-permute-start | bytes 417800 | tf_op jit(solution)/shard_map/ppermute | solution.py:50
  51.1 7.1 %collective-permute-start.16 = (f32[2,68,256]{2,1,0:T(8,128)S(1)}, f32[2,68,256]{2,1,0:T(8,128)S(1)}, u32[]{:S(2)}, u32[]{:S(2)}) collective-permute-start(f32[2,68,256]{2,1,0:T(8,128)S(1)} %get-tuple-element.33), channel_id=1, source_target_pairs={{0,1},{1,0},{2,3},{3,2},{4,5},{5,4},{6,7},{7,6},{8,9},{9,8},{10,11... | collective-permute-start | bytes 417800 | tf_op jit(solution)/shard_map/ppermute | solution.py:37
  58.2 1.2 %gram.1 = f32[264,128]{1,0:T(8,128)S(1)} custom-call(f32[16,64,256]{2,1,0:T(8,128)S(1)} %get-tuple-element.26.extrap_ref.refs_2_, f32[16,64,256]{2,1,0:T(8,128)S(1)} %copy-done), custom_call_target="tpu_custom_call" | custom-call | tf_op jit(solution)/shard_map/gram/pallas_call | solution.py:259
  60.1 5.5 %collective-permute-done.17 = f32[264,128]{1,0:T(8,128)S(1)} collective-permute-done((f32[264,128]{1,0:T(8,128)S(1)}, f32[264,128]{1,0:T(8,128)S(1)}, u32[]{:S(2)}, u32[]{:S(2)}) %collective-permute-start.17) | collective-permute-done | bytes 135200 | tf_op jit(solution)/shard_map/ppermute | solution.py:37
  65.7 2.1 %collective-permute-start.18 = (f32[264,128]{1,0:T(8,128)S(1)}, f32[264,128]{1,0:T(8,128)S(1)}, u32[]{:S(2)}, u32[]{:S(2)}) collective-permute-start(f32[264,128]{1,0:T(8,128)S(1)} %add.97.refs_0_), channel_id=1, source_target_pairs={{0,2},{1,3},{2,0},{3,1},{4,6},{5,7},{6,4},{7,5},{8,10},{9,11},{10,... | collective-permute-start | bytes 405512 | tf_op jit(solution)/shard_map/ppermute | solution.py:37
  67.9 0.1 pad_maximum_fusion
  68.0 0.5 collective-permute-start.24
  68.6 1.5 %collective-permute-start.25 = (bf16[4,128,256]{2,1,0:T(8,128)(2,1)S(1)}, bf16[4,128,256]{2,1,0:T(8,128)(2,1)S(1)}, u32[]{:S(2)}, u32[]{:S(2)}) collective-permute-start(bf16[4,128,256]{2,1,0:T(8,128)(2,1)S(1)} %slice.173), channel_id=1, source_target_pairs={{0,8},{4,12},{8,0},{12,4},{16,24},{20,28},{24,16},{28,20},{1,9},{5... | collective-permute-start | bytes 786440 | tf_op jit(solution)/shard_map/ppermute | solution.py:37
  70.0 5.5 %collective-permute-done.18.refs_1_ = f32[264,128]{1,0:T(8,128)S(1)} collective-permute-done((f32[264,128]{1,0:T(8,128)S(1)}, f32[264,128]{1,0:T(8,128)S(1)}, u32[]{:S(2)}, u32[]{:S(2)}) %collective-permute-start.18) | collective-permute-done | bytes 135200 | tf_op jit(solution)/shard_map/ppermute | solution.py:37
  75.6 0.4 fusion
  76.0 0.6 collective-permute-done.24.refs_6_
  76.6 0.2 collective-permute-done.25.refs_7_
  76.8 0.3 collective-permute-start.27
  77.0 1.6 %fusion.11 = f32[16,64,256]{2,1,0:T(8,128)} fusion(f32[16,64,256]{2,1,0:T(8,128)S(1)} %copy-done.5, f32[16,68,256]{2,1,0:T(8,128)S(1)} %fusion), kind=kLoop, calls=%fused_computation.26 | loop fusion | flops 2621440 | bytes 6291456 | tf_op jit(solution)/shard_map/jit(clip)/min | solution.py:552
  78.6 5.4 %rank.1 = f32[16,64,256]{2,1,0:T(8,128)} custom-call(s32[1]{0:T(128)S(6)} %copy.14.keep_ref, f32[264,128]{1,0:T(8,128)S(1)} %add.97.refs_0_, f32[264,128]{1,0:T(8,128)S(1)} %collective-permute-done.18.refs_1_, f32[16,64,256]{2,1,0:T(8,128)S(1)} %get-tuple-element.26.extrap_ref.refs_2_, f32[16,64,256]{2,1,0:T(8,128)S(1)} %copy-done), custom_call_target="tpu_custom_call" | custom-call | tf_op jit(solution)/shard_map/rank/pallas_call | solution.py:352
  84.1 6.7 %forward.1 = f32[1,2,1024,256]{3,2,1,0:T(8,128)} custom-call(s32[8,2,24]{2,1,0:T(2,128)S(1)} %copy-done.2, s32[2,8]{1,0:T(2,128)S(1)} %bitcast.24, bf16[1,2,24,1024,128]{4,3,2,1,0:T(8,128)(2,1)S(1)} %bitcast.22, f32[1,2,1024,256]{3,2,1,0:T(8,128)} %dual_hbm.3, bf16[1,2,1024,256]{3,2,1,0:T(8,128)(2,1)} %seen_hbm.1, f32[1,2,256]{2,1,0:T(2,128)S(1)} %copy-done.4, ...), custom_call_target="tpu_custom_call" | custom-call | tf_op jit(solution)/shard_map/forward/pallas_call | solution.py:425
  (54 shorter events, 0.4 us)
Async XLA Ops:
  1.6 11.9 %collective-permute-start = (f32[16,2,256]{2,1,0:T(2,128)S(1)}, f32[16,2,256]{2,1,0:T(2,128)S(1)}, u32[]{:S(2)}, u32[]{:S(2)}) collective-permute-start(f32[16,2,256]{2,1,0:T(2,128)S(1)} %get-tuple-element.40), channel_id=1, source_target_pairs={{4,8},{12,16},{20,24},{8,4},{16,12},{24,20},{5,9},{13,17},{21,25},... | collective-permute-start | bytes 98312 | tf_op jit(solution)/shard_map/ppermute | solution.py:50
  2.3 11.2 %collective-permute-start.1 = (f32[16,2,256]{2,1,0:T(2,128)S(1)}, f32[16,2,256]{2,1,0:T(2,128)S(1)}, u32[]{:S(2)}, u32[]{:S(2)}) collective-permute-start(f32[16,2,256]{2,1,0:T(2,128)S(1)} %get-tuple-element.41), channel_id=1, source_target_pairs={{0,4},{4,0},{8,12},{12,8},{16,20},{20,16},{24,28},{28,24},{1,5},{5... | collective-permute-start | bytes 98312 | tf_op jit(solution)/shard_map/ppermute | solution.py:37
  6.7 6.9 %copy-start.5 = (f32[16,64,256]{2,1,0:T(8,128)S(1)}, f32[16,64,256]{2,1,0:T(8,128)}, u32[]{:S(2)}) copy-start(f32[16,64,256]{2,1,0:T(8,128)} %param.11) | copy-start | bytes 3145732
  12.5 9.1 %collective-permute-start.7 = (bf16[8,256,128]{2,1,0:T(8,128)(2,1)S(1)}, bf16[8,256,128]{2,1,0:T(8,128)(2,1)S(1)}, u32[]{:S(2)}, u32[]{:S(2)}) collective-permute-start(bf16[8,256,128]{2,1,0:T(8,128)(2,1)S(1)} %get-tuple-element.24), channel_id=1, source_target_pairs={{0,4},{4,0},{8,12},{12,8},{16,20},{20,16},{24,28},{28,24},{1,5},{5... | collective-permute-start | bytes 1572872 | tf_op jit(solution)/shard_map/ppermute | solution.py:37
  13.8 7.6 %collective-permute-start.2 = (f32[2,68,256]{2,1,0:T(8,128)S(1)}, f32[2,68,256]{2,1,0:T(8,128)S(1)}, u32[]{:S(2)}, u32[]{:S(2)}) collective-permute-start(f32[2,68,256]{2,1,0:T(8,128)S(1)} %get-tuple-element.34), channel_id=1, source_target_pairs={{0,1},{1,0},{2,3},{3,2},{4,5},{5,4},{6,7},{7,6},{8,9},{9,8},{10,11... | collective-permute-start | bytes 417800 | tf_op jit(solution)/shard_map/ppermute | solution.py:37
  16.9 4.5 %collective-permute-start.3 = (f32[2,68,256]{2,1,0:T(8,128)S(1)}, f32[2,68,256]{2,1,0:T(8,128)S(1)}, u32[]{:S(2)}, u32[]{:S(2)}) collective-permute-start(f32[2,68,256]{2,1,0:T(8,128)S(1)} %get-tuple-element.35), channel_id=1, source_target_pairs={{1,2},{2,1},{5,6},{6,5},{9,10},{10,9},{13,14},{14,13},{17,18},{18,... | collective-permute-start | bytes 417800 | tf_op jit(solution)/shard_map/ppermute | solution.py:50
  17.6 13.5 %collective-permute-start.5 = (bf16[2,8,256,128]{3,2,1,0:T(8,128)(2,1)S(1)}, bf16[2,8,256,128]{3,2,1,0:T(8,128)(2,1)S(1)}, u32[]{:S(2)}, u32[]{:S(2)}) collective-permute-start(bf16[2,8,256,128]{3,2,1,0:T(8,128)(2,1)S(1)} %get-tuple-element.22), channel_id=1, source_target_pairs={{0,4},{4,0},{8,12},{12,8},{16,20},{20,16},{24,28},{28,24},{1,5},{5... | collective-permute-start | bytes 3145736 | tf_op jit(solution)/shard_map/ppermute | solution.py:37
  17.8 18.3 %collective-permute-start.4 = (bf16[8,256,128]{2,1,0:T(8,128)(2,1)S(1)}, bf16[8,256,128]{2,1,0:T(8,128)(2,1)S(1)}, u32[]{:S(2)}, u32[]{:S(2)}) collective-permute-start(bf16[8,256,128]{2,1,0:T(8,128)(2,1)S(1)} %get-tuple-element.20), channel_id=1, source_target_pairs={{0,4},{4,0},{8,12},{12,8},{16,20},{20,16},{24,28},{28,24},{1,5},{5... | collective-permute-start | bytes 1572872 | tf_op jit(solution)/shard_map/ppermute | solution.py:37
  21.7 8.2 %collective-permute-start.10 = (bf16[4,256,128]{2,1,0:T(8,128)(2,1)S(1)}, bf16[4,256,128]{2,1,0:T(8,128)(2,1)S(1)}, u32[]{:S(2)}, u32[]{:S(2)}) collective-permute-start(bf16[4,256,128]{2,1,0:T(8,128)(2,1)S(1)} %get-tuple-element.38), channel_id=1, source_target_pairs={{0,16},{4,20},{8,24},{12,28},{16,0},{20,4},{24,8},{28,12},{1,17},{... | collective-permute-start | bytes 786440 | tf_op jit(solution)/shard_map/ppermute | solution.py:37
  23.5 7.6 %collective-permute-start.8 = (bf16[4,256,128]{2,1,0:T(8,128)(2,1)S(1)}, bf16[4,256,128]{2,1,0:T(8,128)(2,1)S(1)}, u32[]{:S(2)}, u32[]{:S(2)}) collective-permute-start(bf16[4,256,128]{2,1,0:T(8,128)(2,1)S(1)} %get-tuple-element.39), channel_id=1, source_target_pairs={{0,8},{4,12},{8,0},{12,4},{16,24},{20,28},{24,16},{28,20},{1,9},{5... | collective-permute-start | bytes 786440 | tf_op jit(solution)/shard_map/ppermute | solution.py:37
  31.0 4.6 %copy-start.1 = (f32[16,64,256]{2,1,0:T(8,128)S(1)}, f32[16,64,256]{2,1,0:T(8,128)}, u32[]{:S(2)}) copy-start(f32[16,64,256]{2,1,0:T(8,128)} %refs_0_.1) | copy-start | bytes 3145732
  31.2 4.3 %copy-start = (f32[16,64,256]{2,1,0:T(8,128)S(1)}, f32[16,64,256]{2,1,0:T(8,128)}, u32[]{:S(2)}) copy-start(f32[16,64,256]{2,1,0:T(8,128)} %refs_3_.1) | copy-start | bytes 3145732
  31.3 9.2 %collective-permute-start.11 = (bf16[4,256,128]{2,1,0:T(8,128)(2,1)S(1)}, bf16[4,256,128]{2,1,0:T(8,128)(2,1)S(1)}, u32[]{:S(2)}, u32[]{:S(2)}) collective-permute-start(bf16[4,256,128]{2,1,0:T(8,128)(2,1)S(1)} %get-tuple-element.30), channel_id=1, source_target_pairs={{0,8},{4,12},{8,0},{12,4},{16,24},{20,28},{24,16},{28,20},{1,9},{5... | collective-permute-start | bytes 786440 | tf_op jit(solution)/shard_map/ppermute | solution.py:37
  31.6 9.2 %collective-permute-start.9 = (bf16[4,256,128]{2,1,0:T(8,128)(2,1)S(1)}, bf16[4,256,128]{2,1,0:T(8,128)(2,1)S(1)}, u32[]{:S(2)}, u32[]{:S(2)}) collective-permute-start(bf16[4,256,128]{2,1,0:T(8,128)(2,1)S(1)} %get-tuple-element.31), channel_id=1, source_target_pairs={{0,16},{4,20},{8,24},{12,28},{16,0},{20,4},{24,8},{28,12},{1,17},{... | collective-permute-start | bytes 786440 | tf_op jit(solution)/shard_map/ppermute | solution.py:37
  33.1 10.8 %collective-permute-start.12 = (bf16[4,256,128]{2,1,0:T(8,128)(2,1)S(1)}, bf16[4,256,128]{2,1,0:T(8,128)(2,1)S(1)}, u32[]{:S(2)}, u32[]{:S(2)}) collective-permute-start(bf16[4,256,128]{2,1,0:T(8,128)(2,1)S(1)} %get-tuple-element.28), channel_id=1, source_target_pairs={{0,16},{4,20},{8,24},{12,28},{16,0},{20,4},{24,8},{28,12},{1,17},{... | collective-permute-start | bytes 786440 | tf_op jit(solution)/shard_map/ppermute | solution.py:37
  33.8 10.1 %collective-permute-start.6 = (bf16[4,256,128]{2,1,0:T(8,128)(2,1)S(1)}, bf16[4,256,128]{2,1,0:T(8,128)(2,1)S(1)}, u32[]{:S(2)}, u32[]{:S(2)}) collective-permute-start(bf16[4,256,128]{2,1,0:T(8,128)(2,1)S(1)} %get-tuple-element.29), channel_id=1, source_target_pairs={{0,8},{4,12},{8,0},{12,4},{16,24},{20,28},{24,16},{28,20},{1,9},{5... | collective-permute-start | bytes 786440 | tf_op jit(solution)/shard_map/ppermute | solution.py:37
  45.4 4.5 %collective-permute-start.13 = (f32[16,2,256]{2,1,0:T(2,128)S(1)}, f32[16,2,256]{2,1,0:T(2,128)S(1)}, u32[]{:S(2)}, u32[]{:S(2)}) collective-permute-start(f32[16,2,256]{2,1,0:T(2,128)S(1)} %get-tuple-element.36), channel_id=1, source_target_pairs={{4,8},{12,16},{20,24},{8,4},{16,12},{24,20},{5,9},{13,17},{21,25},... | collective-permute-start | bytes 98312 | tf_op jit(solution)/shard_map/ppermute | solution.py:50
  46.1 3.9 %collective-permute-start.14 = (f32[16,2,256]{2,1,0:T(2,128)S(1)}, f32[16,2,256]{2,1,0:T(2,128)S(1)}, u32[]{:S(2)}, u32[]{:S(2)}) collective-permute-start(f32[16,2,256]{2,1,0:T(2,128)S(1)} %get-tuple-element.37), channel_id=1, source_target_pairs={{0,4},{4,0},{8,12},{12,8},{16,20},{20,16},{24,28},{28,24},{1,5},{5... | collective-permute-start | bytes 98312 | tf_op jit(solution)/shard_map/ppermute | solution.py:37
  49.0 19.0 %collective-permute-start.20 = (bf16[8,128,256]{2,1,0:T(8,128)(2,1)S(1)}, bf16[8,128,256]{2,1,0:T(8,128)(2,1)S(1)}, u32[]{:S(2)}, u32[]{:S(2)}) collective-permute-start(bf16[8,128,256]{2,1,0:T(8,128)(2,1)S(1)} %get-tuple-element.27.refs_0_), channel_id=1, source_target_pairs={{0,8},{4,12},{8,0},{12,4},{16,24},{20,28},{24,16},{28,20},{1,9},{5... | collective-permute-start | bytes 1572872 | tf_op jit(solution)/shard_map/ppermute | solution.py:37
  49.9 18.6 %collective-permute-start.22 = (bf16[8,128,256]{2,1,0:T(8,128)(2,1)S(1)}, bf16[8,128,256]{2,1,0:T(8,128)(2,1)S(1)}, u32[]{:S(2)}, u32[]{:S(2)}) collective-permute-start(bf16[8,128,256]{2,1,0:T(8,128)(2,1)S(1)} %get-tuple-element.27.refs_0_), channel_id=1, source_target_pairs={{0,16},{4,20},{8,24},{12,28},{16,0},{20,4},{24,8},{28,12},{1,17},{... | collective-permute-start | bytes 1572872 | tf_op jit(solution)/shard_map/ppermute | solution.py:37
  49.9 34.1 %slice-start = ((s8[12582912]{0:T(1024)(128)(4,1)}), s8[4194304]{0:T(1024)(128)(4,1)S(1)}, s32[]{:S(2)}) async-start(s8[12582912]{0:T(1024)(128)(4,1)} %bitcast.21), calls=%async_computation | async-start | bytes 8388608
  50.1 15.6 %collective-permute-start.15 = (f32[2,68,256]{2,1,0:T(8,128)S(1)}, f32[2,68,256]{2,1,0:T(8,128)S(1)}, u32[]{:S(2)}, u32[]{:S(2)}) collective-permute-start(f32[2,68,256]{2,1,0:T(8,128)S(1)} %get-tuple-element.32), channel_id=1, source_target_pairs={{1,2},{2,1},{5,6},{6,5},{9,10},{10,9},{13,14},{14,13},{17,18},{18,... | collective-permute-start | bytes 417800 | tf_op jit(solution)/shard_map/ppermute | solution.py:50
  51.1 16.7 %collective-permute-start.16 = (f32[2,68,256]{2,1,0:T(8,128)S(1)}, f32[2,68,256]{2,1,0:T(8,128)S(1)}, u32[]{:S(2)}, u32[]{:S(2)}) collective-permute-start(f32[2,68,256]{2,1,0:T(8,128)S(1)} %get-tuple-element.33), channel_id=1, source_target_pairs={{0,1},{1,0},{2,3},{3,2},{4,5},{5,4},{6,7},{7,6},{8,9},{9,8},{10,11... | collective-permute-start | bytes 417800 | tf_op jit(solution)/shard_map/ppermute | solution.py:37
  59.4 6.3 %collective-permute-start.17 = (f32[264,128]{1,0:T(8,128)S(1)}, f32[264,128]{1,0:T(8,128)S(1)}, u32[]{:S(2)}, u32[]{:S(2)}) collective-permute-start(f32[264,128]{1,0:T(8,128)S(1)} %gram.1), channel_id=1, source_target_pairs={{0,1},{1,0},{2,3},{3,2},{4,5},{5,4},{6,7},{7,6},{8,9},{9,8},{10,11... | collective-permute-start | bytes 405512 | tf_op jit(solution)/shard_map/ppermute | solution.py:37
  65.7 18.3 %collective-permute-start.19 = (bf16[8,128,256]{2,1,0:T(8,128)(2,1)S(1)}, bf16[8,128,256]{2,1,0:T(8,128)(2,1)S(1)}, u32[]{:S(2)}, u32[]{:S(2)}) collective-permute-start(bf16[8,128,256]{2,1,0:T(8,128)(2,1)S(1)} %get-tuple-element.27.refs_0_), channel_id=1, source_target_pairs={{0,4},{4,0},{8,12},{12,8},{16,20},{20,16},{24,28},{28,24},{1,5},{5... | collective-permute-start | bytes 1572872 | tf_op jit(solution)/shard_map/ppermute | solution.py:37
  65.7 9.9 %collective-permute-start.18 = (f32[264,128]{1,0:T(8,128)S(1)}, f32[264,128]{1,0:T(8,128)S(1)}, u32[]{:S(2)}, u32[]{:S(2)}) collective-permute-start(f32[264,128]{1,0:T(8,128)S(1)} %add.97.refs_0_), channel_id=1, source_target_pairs={{0,2},{1,3},{2,0},{3,1},{4,6},{5,7},{6,4},{7,5},{8,10},{9,11},{10,... | collective-permute-start | bytes 405512 | tf_op jit(solution)/shard_map/ppermute | solution.py:37
  67.8 16.3 %slice-start.1 = ((s8[12582912]{0:T(1024)(128)(4,1)}), s8[4194304]{0:T(1024)(128)(4,1)S(1)}, s32[]{:S(2)}) async-start(s8[12582912]{0:T(1024)(128)(4,1)} %bitcast.21), calls=%async_computation.1 | async-start | bytes 8388608
  68.0 8.5 %collective-permute-start.24 = (bf16[4,128,256]{2,1,0:T(8,128)(2,1)S(1)}, bf16[4,128,256]{2,1,0:T(8,128)(2,1)S(1)}, u32[]{:S(2)}, u32[]{:S(2)}) collective-permute-start(bf16[4,128,256]{2,1,0:T(8,128)(2,1)S(1)} %slice.172), channel_id=1, source_target_pairs={{0,16},{4,20},{8,24},{12,28},{16,0},{20,4},{24,8},{28,12},{1,17},{... | collective-permute-start | bytes 786440 | tf_op jit(solution)/shard_map/ppermute | solution.py:37
  68.6 8.2 %collective-permute-start.25 = (bf16[4,128,256]{2,1,0:T(8,128)(2,1)S(1)}, bf16[4,128,256]{2,1,0:T(8,128)(2,1)S(1)}, u32[]{:S(2)}, u32[]{:S(2)}) collective-permute-start(bf16[4,128,256]{2,1,0:T(8,128)(2,1)S(1)} %slice.173), channel_id=1, source_target_pairs={{0,8},{4,12},{8,0},{12,4},{16,24},{20,28},{24,16},{28,20},{1,9},{5... | collective-permute-start | bytes 786440 | tf_op jit(solution)/shard_map/ppermute | solution.py:37
  70.0 14.0 %collective-permute-start.21 = (bf16[8,128,256]{2,1,0:T(8,128)(2,1)S(1)}, bf16[8,128,256]{2,1,0:T(8,128)(2,1)S(1)}, u32[]{:S(2)}, u32[]{:S(2)}) collective-permute-start(bf16[8,128,256]{2,1,0:T(8,128)(2,1)S(1)} %collective-permute-done.20.refs_2_), channel_id=1, source_target_pairs={{0,4},{4,0},{8,12},{12,8},{16,20},{20,16},{24,28},{28,24},{1,5},{5... | collective-permute-start | bytes 1572872 | tf_op jit(solution)/shard_map/ppermute | solution.py:37
  75.6 8.5 %collective-permute-start.23 = (bf16[8,128,256]{2,1,0:T(8,128)(2,1)S(1)}, bf16[8,128,256]{2,1,0:T(8,128)(2,1)S(1)}, u32[]{:S(2)}, u32[]{:S(2)}) collective-permute-start(bf16[8,128,256]{2,1,0:T(8,128)(2,1)S(1)} %collective-permute-done.22.refs_4_), channel_id=1, source_target_pairs={{0,4},{4,0},{8,12},{12,8},{16,20},{20,16},{24,28},{28,24},{1,5},{5... | collective-permute-start | bytes 1572872 | tf_op jit(solution)/shard_map/ppermute | solution.py:37
  76.0 8.1 %slice-start.2 = ((s8[12582912]{0:T(1024)(128)(4,1)}), s8[4194304]{0:T(1024)(128)(4,1)S(1)}, s32[]{:S(2)}) async-start(s8[12582912]{0:T(1024)(128)(4,1)} %bitcast.21), calls=%async_computation.2 | async-start | bytes 8388608
  76.5 7.5 %collective-permute-start.26 = (bf16[4,128,256]{2,1,0:T(8,128)(2,1)S(1)}, bf16[4,128,256]{2,1,0:T(8,128)(2,1)S(1)}, u32[]{:S(2)}, u32[]{:S(2)}) collective-permute-start(bf16[4,128,256]{2,1,0:T(8,128)(2,1)S(1)} %collective-permute-done.24.refs_6_), channel_id=1, source_target_pairs={{0,4},{4,0},{8,12},{12,8},{16,20},{20,16},{24,28},{28,24},{1,5},{5... | collective-permute-start | bytes 786440 | tf_op jit(solution)/shard_map/ppermute | solution.py:37
  76.8 7.3 %collective-permute-start.27 = (bf16[4,128,256]{2,1,0:T(8,128)(2,1)S(1)}, bf16[4,128,256]{2,1,0:T(8,128)(2,1)S(1)}, u32[]{:S(2)}, u32[]{:S(2)}) collective-permute-start(bf16[4,128,256]{2,1,0:T(8,128)(2,1)S(1)} %collective-permute-done.25.refs_7_), channel_id=1, source_target_pairs={{0,4},{4,0},{8,12},{12,8},{16,20},{20,16},{24,28},{28,24},{1,5},{5... | collective-permute-start | bytes 786440 | tf_op jit(solution)/shard_map/ppermute | solution.py:37
  78.6 5.5 %copy-start.2 = (s32[8,2,24]{2,1,0:T(2,128)S(1)}, s32[8,2,24]{2,1,0:T(2,128)}, u32[]{:S(2)}) copy-start(s32[8,2,24]{2,1,0:T(2,128)} %tiles) | copy-start | bytes 4612
  78.6 5.5 %copy-start.3 = (s32[8,2]{0,1:T(2,128)S(1)}, s32[8,2]{0,1:T(2,128)}, u32[]{:S(2)}) copy-start(s32[8,2]{0,1:T(2,128)} %param.18) | copy-start | bytes 196
  78.6 5.5 %copy-start.4 = (f32[1,2,256]{2,1,0:T(2,128)S(1)}, f32[1,2,256]{2,1,0:T(2,128)}, u32[]{:S(2)}) copy-start(f32[1,2,256]{2,1,0:T(2,128)} %radius_ref.1) | copy-start | bytes 6148

commit v2 on v1

--- a/solution.py
+++ b/solution.py
@@ -200,7 +200,7 @@
 def primal_body(*refs, parts):
     sky_ref, base_ref, rest_ref, own_ref, mate_ref = refs[:5]
     halves = (refs[5 : 5 + parts], refs[5 + parts : 5 + 2 * parts])
-    next_ref, extrap_ref, tiles_ref = refs[5 + 2 * parts :]
+    extrap_ref, tiles_ref = refs[5 + 2 * parts :]
     _, columns, channels = sky_ref.shape
     across = columns // TC
     half = tiles_ref.shape[0] // 2
@@ -218,7 +218,6 @@
                 base_ref[rows, cols, :] - step_primal * (back + rest_ref[rows, cols, :]), 0.0
             )
             extrap = 2.0 * new - sky
-            next_ref[rows, cols, :] = new
             extrap_ref[rows, cols, :] = extrap
             tiles_ref[tile] = extrap.reshape(TR * TC, channels).astype(jnp.bfloat16)
 
@@ -228,9 +227,9 @@
     tiles = jax.ShapeDtypeStruct((own.shape[0], own.shape[2], own.shape[1]), jnp.bfloat16)
     return pl.pallas_call(
         functools.partial(primal_body, parts=len(low)),
-        out_shape=[whole, whole, tiles],
+        out_shape=[whole, tiles],
         in_specs=[vmem_spec] * (5 + len(low) + len(high)),
-        out_specs=[vmem_spec] * 3,
+        out_specs=[vmem_spec] * 2,
         compiler_params=pltpu.CompilerParams(vmem_limit_bytes=16 * MIB),
         name="primal",
     )(sky, base, rest, own, mate, *low, *high)
@@ -295,7 +294,7 @@
 
 def rank_body(keep_ref, *refs, parts):
     packed_refs = refs[:parts]
-    extrap_hbm, rank_hbm, out_ref, extrap_buf, rank_buf, sems = refs[parts:]
+    extrap_hbm, rank_hbm, out_hbm, extrap_buf, rank_buf, out_buf, sems = refs[parts:]
     loads = [
         pltpu.make_async_copy(extrap_hbm, extrap_buf, sems.at[0]),
         pltpu.make_async_copy(rank_hbm, rank_buf, sems.at[1]),
@@ -344,8 +343,21 @@
     inverse = inverse + dot_fine(inverse, residual)
     for load in loads:
         load.wait()
-    mixed = (rank_buf[...] + step_rank * extrap_buf[...]).reshape(height * columns, channels)
-    out_ref[...] = dot_fine(mixed, inverse).reshape(height, columns, channels)
+    high, low = split(inverse)
+    right = jnp.concatenate([high, low, high], axis=0)
+    stores = []
+    share = height // 4
+    for i in range(4):
+        rows = pl.ds(i * share, share)
+        mixed = (rank_buf[rows] + step_rank * extrap_buf[rows]).reshape(share * columns, channels)
+        high, low = split(mixed)
+        left = jnp.concatenate([high, high, low], axis=1)
+        product = jnp.dot(left, right, preferred_element_type=jnp.float32)
+        out_buf[rows] = product.reshape(share, columns, channels)
+        stores.append(pltpu.make_async_copy(out_buf.at[rows], out_hbm.at[rows], sems.at[2 + i]))
+        stores[i].start()
+    for store in stores:
+        store.wait()
 
 
 def rank_update(keep_count, packed, extrap, rank_dual):
@@ -353,13 +365,14 @@
         functools.partial(rank_body, parts=len(packed)),
         out_shape=jax.ShapeDtypeStruct(extrap.shape, jnp.float32),
         in_specs=[smem_spec] + [vmem_spec] * len(packed) + [any_spec, any_spec],
-        out_specs=vmem_spec,
+        out_specs=hbm_spec,
         scratch_shapes=[
             pltpu.VMEM(extrap.shape, jnp.float32),
             pltpu.VMEM(extrap.shape, jnp.float32),
-            pltpu.SemaphoreType.DMA((2,)),
+            pltpu.VMEM(extrap.shape, jnp.float32),
+            pltpu.SemaphoreType.DMA((6,)),
         ],
-        compiler_params=pltpu.CompilerParams(vmem_limit_bytes=12 * MIB),
+        compiler_params=pltpu.CompilerParams(vmem_limit_bytes=14 * MIB),
         name="rank",
     )(keep_count, *packed, extrap, rank_dual)
 
@@ -369,7 +382,7 @@
 ):
     image_refs, out_hbm = refs[:-8], refs[-8]
     image, acc, dual, seen, image_sems, load_sems, store_sems = refs[-7:]
-    blocks, depth, _, _ = degrid_ref.shape[1:5]
+    blocks, depth, entries, _ = degrid_ref.shape[1:5]
     me = lax.axis_index("facet")
     images = []
     live = 0
@@ -379,8 +392,15 @@
             pltpu.make_async_copy(ref, image.at[pl.ds(live, size)], image_sems.at[i])
         )
         live += size
+    cut = entries // 4
     stores = [
-        pltpu.make_async_copy(acc.at[b], out_hbm.at[0, b], store_sems.at[b]) for b in range(blocks)
+        [
+            pltpu.make_async_copy(
+                acc.at[b, pl.ds(i * cut, cut)], out_hbm.at[0, b, pl.ds(i * cut, cut)], store_sems.at[b, i]
+            )
+            for i in range(4)
+        ]
+        for b in range(blocks)
     ]
     loads = [
         pltpu.make_async_copy(dual_hbm.at[0], dual, load_sems.at[0]),
@@ -412,10 +432,12 @@
         misfit = acc[b] + (dual[b] - seen[b].astype(jnp.float32))
         size = jnp.sqrt(jnp.sum(misfit * misfit, axis=0, keepdims=True) + 1e-06)
         scale = jnp.maximum(0.0, 1.0 - radius_ref[0, b : b + 1, :] / size)
-        acc[b] = misfit * scale
-        stores[b].start()
-    for copy in stores:
-        copy.wait()
+        for i in range(4):
+            acc[b, i * cut : (i + 1) * cut] = misfit[i * cut : (i + 1) * cut] * scale
+            stores[b][i].start()
+    for b in range(blocks):
+        for copy in stores[b]:
+            copy.wait()
 
 
 def forward(tile_list, counts, degrid, dual, observed, radius, image, chips, tile_count):
@@ -435,7 +457,7 @@
             pltpu.VMEM((blocks, entries, channels), jnp.bfloat16),
             pltpu.SemaphoreType.DMA((len(image),)),
             pltpu.SemaphoreType.DMA((2,)),
-            pltpu.SemaphoreType.DMA((blocks,)),
+            pltpu.SemaphoreType.DMA((blocks, 4)),
         ],
         compiler_params=pltpu.CompilerParams(vmem_limit_bytes=forward_limit * MIB),
         name="forward",
@@ -544,7 +566,9 @@
     wave_halo = padded_2(wave_dual, sides, 2)
     base = sky_image - step_primal * rank_dual
     rest = synthesis(wave_halo, height, columns)
-    sky_next, extrap, tiles = primal(sky_image, base, rest, sums[2], mate_own, low, high)
+    extrap, tiles = primal(sky_image, base, rest, sums[2], mate_own, low, high)
+
+    sky_next = 0.5 * (extrap + sky_image)
 
     image = from_owners(tiles, chips)
     packed = gram_of(extrap, rank_dual)

time: 91.2 us -> 86.7 us (0.951)
  waiting for transfers between devices: 30.1 us -> 22.5 us
  starting transfers between devices: 33.5 us -> 35.9 us
  Pallas kernels: 20.6 us -> 19.4 us
  other arithmetic: 4.99 us -> 6.1 us
    ppermute x24, waiting for transfers between devices: 30.1 us -> 22.5 us  [swap(): return lax.ppermute(value, axis, [(i, i ^ mask) for i in range(count)])]
    ppermute x24, starting transfers between devices: 30.5 us -> 33 us  [swap(): return lax.ppermute(value, axis, [(i, i ^ mask) for i in range(count)])]
    mul x0 -> x1, other arithmetic: none -> 1.11 us  [iteration(): sky_next = 0.5 * (extrap + sky_image)]
    pallas_call x1, Pallas kernels: 1.45 us -> 0.48 us  [primal(): pl.pallas_call(functools.partial(primal_body, parts=len(low)), out_shape=...]
  transfers between devices with their start and end apart: 28 -> 28, of which waited for: 10 -> 9; matrix products, arithmetic and copies ran while one was open for 4% -> 6% of each run, Pallas kernels for 14% -> 14%
where the time goes in v2:
time: 86.7 us; the launch traced here: 85.8 us
  starting transfers between devices  35.9 us (41%)
  waiting for transfers between devices  22.5 us (26%)
  Pallas kernels  19.4 us (22%)
  other arithmetic  6.1 us (7%)
  between operations  1.83 us (2%)
    ppermute x24, starting transfers between devices, swap(): return lax.ppermute(value, axis, [(i, i ^ mask) for i in range(count)])  33 us
    ppermute x24, waiting for transfers between devices, swap(): return lax.ppermute(value, axis, [(i, i ^ mask) for i in range(count)])  22.5 us
    pallas_call x1, Pallas kernels, forward(): pl.pallas_call(functools.partial(forward_body, chips=chips, tile_count=ti...  6.72 us
    pallas_call x1, Pallas kernels, adjoint(): pl.pallas_call(functools.partial(adjoint_body, chips=chips, tile_count=ti...  5.77 us
    pallas_call x1, Pallas kernels, rank_update(): pl.pallas_call(functools.partial(rank_body, parts=len(packed)), out_shape...  5.18 us
    ppermute x4, starting transfers between devices, padded_2(): outside = lax.ppermute(outward, axis, outer)  2.97 us
  transfers between devices with their start and end apart: 28, of which 9 were waited for; matrix products, arithmetic and copies ran while one was open for 6% of the time, Pallas kernels for 14%

profile of v2, /device:TPU:0, one launch (start us, length us, event | category | flops | bytes accessed | tf_op | source)
XLA Modules:
  0.0 85.8 jit_solution(15809412638276709133)
XLA Ops:
  0.6 1.0 %broadcast_select_fusion.11 = (f32[16,2,256]{2,1,0:T(2,128)S(1)}, f32[16,2,256]{2,1,0:T(2,128)S(1)}) fusion(pred[]{:T(512)S(6)} %eq.6, f32[16,64,256]{2,1,0:T(8,128)} %param.11), kind=kLoop, calls=%fused_computation.66 | loop fusion | flops 16384 | bytes 131073 | tf_op jit(solution)/shard_map/jit(_where)/select_n | solution.py:48
  1.6 0.7 collective-permute-start
  2.3 4.4 %collective-permute-start.1 = (f32[16,2,256]{2,1,0:T(2,128)S(1)}, f32[16,2,256]{2,1,0:T(2,128)S(1)}, u32[]{:S(2)}, u32[]{:S(2)}) collective-permute-start(f32[16,2,256]{2,1,0:T(2,128)S(1)} %get-tuple-element.39), channel_id=1, source_target_pairs={{0,4},{4,0},{8,12},{12,8},{16,20},{20,16},{24,28},{28,24},{1,5},{5... | collective-permute-start | bytes 98312 | tf_op jit(solution)/shard_map/ppermute | solution.py:37
  6.7 5.8 %adjoint.1 = (bf16[8,256,128]{2,1,0:T(8,128)(2,1)S(1)}, bf16[2,8,256,128]{3,2,1,0:T(8,128)(2,1)S(1)}, bf16[8,256,128]{2,1,0:T(8,128)(2,1)S(1)}, bf16[8,256,128]{...) custom-call(s32[8,2,24]{2,1,0:T(2,128)} %tiles, s32[2,8]{1,0:T(2,128)} %bitcast.23, ...), custom_call_target="tpu_custom_call" | custom-call | tf_op jit(solution)/shard_map/adjoint/pallas_call | solution.py:179
  12.5 1.1 %collective-permute-start.7 = (bf16[8,256,128]{2,1,0:T(8,128)(2,1)S(1)}, bf16[8,256,128]{2,1,0:T(8,128)(2,1)S(1)}, u32[]{:S(2)}, u32[]{:S(2)}) collective-permute-start(bf16[8,256,128]{2,1,0:T(8,128)(2,1)S(1)} %get-tuple-element.23), channel_id=1, source_target_pairs={{0,4},{4,0},{8,12},{12,8},{16,20},{20,16},{24,28},{28,24},{1,5},{5... | collective-permute-start | bytes 1572872 | tf_op jit(solution)/shard_map/ppermute | solution.py:37
  13.6 0.1 pad_maximum_fusion.7
  13.8 3.2 %collective-permute-start.2 = (f32[2,68,256]{2,1,0:T(8,128)S(1)}, f32[2,68,256]{2,1,0:T(8,128)S(1)}, u32[]{:S(2)}, u32[]{:S(2)}) collective-permute-start(f32[2,68,256]{2,1,0:T(8,128)S(1)} %get-tuple-element.32), channel_id=1, source_target_pairs={{0,1},{1,0},{2,3},{3,2},{4,5},{5,4},{6,7},{7,6},{8,9},{9,8},{10,11... | collective-permute-start | bytes 417800 | tf_op jit(solution)/shard_map/ppermute | solution.py:37
  16.9 0.7 collective-permute-start.3
  17.6 0.3 collective-permute-start.5
  17.8 0.3 collective-permute-start.4
  18.2 3.2 %collective-permute-done.2 = f32[2,68,256]{2,1,0:T(8,128)S(1)} collective-permute-done((f32[2,68,256]{2,1,0:T(8,128)S(1)}, f32[2,68,256]{2,1,0:T(8,128)S(1)}, u32[]{:S(2)}, u32[]{:S(2)}) %collective-permute-start.2) | collective-permute-done | bytes 139296 | tf_op jit(solution)/shard_map/ppermute | solution.py:37
  21.4 0.1 maximum_maximum_fusion
  21.6 0.1 add_convert_fusion.1
  21.7 1.7 %collective-permute-start.10 = (bf16[4,256,128]{2,1,0:T(8,128)(2,1)S(1)}, bf16[4,256,128]{2,1,0:T(8,128)(2,1)S(1)}, u32[]{:S(2)}, u32[]{:S(2)}) collective-permute-start(bf16[4,256,128]{2,1,0:T(8,128)(2,1)S(1)} %get-tuple-element.36), channel_id=1, source_target_pairs={{0,16},{4,20},{8,24},{12,28},{16,0},{20,4},{24,8},{28,12},{1,17},{... | collective-permute-start | bytes 786440 | tf_op jit(solution)/shard_map/ppermute | solution.py:37
  23.5 0.4 fusion.4
  23.9 6.0 %collective-permute-done.10 = bf16[4,256,128]{2,1,0:T(8,128)(2,1)S(1)} collective-permute-done((bf16[4,256,128]{2,1,0:T(8,128)(2,1)S(1)}, bf16[4,256,128]{2,1,0:T(8,128)(2,1)S(1)}, u32[]{:S(2)}, u32[]{:S(2)}) %collective-permute-start.10) | collective-permute-done | bytes 262176 | tf_op jit(solution)/shard_map/ppermute | solution.py:37
  29.9 1.1 %collective-permute-done.8 = bf16[4,256,128]{2,1,0:T(8,128)(2,1)S(1)} collective-permute-done((bf16[4,256,128]{2,1,0:T(8,128)(2,1)S(1)}, bf16[4,256,128]{2,1,0:T(8,128)(2,1)S(1)}, u32[]{:S(2)}, u32[]{:S(2)}) %collective-permute-start.8) | collective-permute-done | bytes 262176 | tf_op jit(solution)/shard_map/ppermute | solution.py:37
  31.0 0.2 fusion.17
  31.3 0.3 collective-permute-start.11
  31.6 1.4 %collective-permute-start.9 = (bf16[4,256,128]{2,1,0:T(8,128)(2,1)S(1)}, bf16[4,256,128]{2,1,0:T(8,128)(2,1)S(1)}, u32[]{:S(2)}, u32[]{:S(2)}) collective-permute-start(bf16[4,256,128]{2,1,0:T(8,128)(2,1)S(1)} %get-tuple-element.29), channel_id=1, source_target_pairs={{0,16},{4,20},{8,24},{12,28},{16,0},{20,4},{24,8},{28,12},{1,17},{... | collective-permute-start | bytes 786440 | tf_op jit(solution)/shard_map/ppermute | solution.py:37
  33.0 0.1 fusion.20
  33.1 0.7 collective-permute-start.12
  33.8 1.7 %collective-permute-start.6 = (bf16[4,256,128]{2,1,0:T(8,128)(2,1)S(1)}, bf16[4,256,128]{2,1,0:T(8,128)(2,1)S(1)}, u32[]{:S(2)}, u32[]{:S(2)}) collective-permute-start(bf16[4,256,128]{2,1,0:T(8,128)(2,1)S(1)} %get-tuple-element.27), channel_id=1, source_target_pairs={{0,8},{4,12},{8,0},{12,4},{16,24},{20,28},{24,16},{28,20},{1,9},{5... | collective-permute-start | bytes 786440 | tf_op jit(solution)/shard_map/ppermute | solution.py:37
  35.6 0.5 fusion.14
  36.1 4.4 %collective-permute-done.11.refs_7_ = bf16[4,256,128]{2,1,0:T(8,128)(2,1)S(1)} collective-permute-done((bf16[4,256,128]{2,1,0:T(8,128)(2,1)S(1)}, bf16[4,256,128]{2,1,0:T(8,128)(2,1)S(1)}, u32[]{:S(2)}, u32[]{:S(2)}) %collective-permute-start.11) | collective-permute-done | bytes 262176 | tf_op jit(solution)/shard_map/ppermute | solution.py:37
  40.5 0.3 collective-permute-done.9.refs_6_
  40.8 3.1 %collective-permute-done.12.refs_8_ = bf16[4,256,128]{2,1,0:T(8,128)(2,1)S(1)} collective-permute-done((bf16[4,256,128]{2,1,0:T(8,128)(2,1)S(1)}, bf16[4,256,128]{2,1,0:T(8,128)(2,1)S(1)}, u32[]{:S(2)}, u32[]{:S(2)}) %collective-permute-start.12) | collective-permute-done | bytes 262176 | tf_op jit(solution)/shard_map/ppermute | solution.py:37
  43.9 0.5 primal.1
  44.4 0.7 collective-permute-start.13
  45.1 2.9 %collective-permute-start.14 = (f32[16,2,256]{2,1,0:T(2,128)S(1)}, f32[16,2,256]{2,1,0:T(2,128)S(1)}, u32[]{:S(2)}, u32[]{:S(2)}) collective-permute-start(f32[16,2,256]{2,1,0:T(2,128)S(1)} %get-tuple-element.35), channel_id=1, source_target_pairs={{0,4},{4,0},{8,12},{12,8},{16,20},{20,16},{24,28},{28,24},{1,5},{5... | collective-permute-start | bytes 98312 | tf_op jit(solution)/shard_map/ppermute | solution.py:37
  48.7 1.0 %collective-permute-start.20 = (bf16[8,128,256]{2,1,0:T(8,128)(2,1)S(1)}, bf16[8,128,256]{2,1,0:T(8,128)(2,1)S(1)}, u32[]{:S(2)}, u32[]{:S(2)}) collective-permute-start(bf16[8,128,256]{2,1,0:T(8,128)(2,1)S(1)} %get-tuple-element.25.refs_0_), channel_id=1, source_target_pairs={{0,8},{4,12},{8,0},{12,4},{16,24},{20,28},{24,16},{28,20},{1,9},{5... | collective-permute-start | bytes 1572872 | tf_op jit(solution)/shard_map/ppermute | solution.py:37
  49.7 1.2 %gram.1 = f32[264,128]{1,0:T(8,128)S(1)} custom-call(f32[16,64,256]{2,1,0:T(8,128)S(1)} %get-tuple-element.24.extrap_ref.refs_2_, f32[16,64,256]{2,1,0:T(8,128)S(1)} %copy-done.1), custom_call_target="tpu_custom_call" | custom-call | tf_op jit(solution)/shard_map/gram/pallas_call | solution.py:258
  50.9 4.4 %collective-permute-start.17 = (f32[264,128]{1,0:T(8,128)S(1)}, f32[264,128]{1,0:T(8,128)S(1)}, u32[]{:S(2)}, u32[]{:S(2)}) collective-permute-start(f32[264,128]{1,0:T(8,128)S(1)} %gram.1), channel_id=1, source_target_pairs={{0,1},{1,0},{2,3},{3,2},{4,5},{5,4},{6,7},{7,6},{8,9},{9,8},{10,11... | collective-permute-start | bytes 405512 | tf_op jit(solution)/shard_map/ppermute | solution.py:37
  55.5 1.0 %collective-permute-start.15 = (f32[2,68,256]{2,1,0:T(8,128)S(1)}, f32[2,68,256]{2,1,0:T(8,128)S(1)}, u32[]{:S(2)}, u32[]{:S(2)}) collective-permute-start(f32[2,68,256]{2,1,0:T(8,128)S(1)} %get-tuple-element.30), channel_id=1, source_target_pairs={{1,2},{2,1},{5,6},{6,5},{9,10},{10,9},{13,14},{14,13},{17,18},{18,... | collective-permute-start | bytes 417800 | tf_op jit(solution)/shard_map/ppermute | solution.py:50
  56.5 2.6 %collective-permute-start.16 = (f32[2,68,256]{2,1,0:T(8,128)S(1)}, f32[2,68,256]{2,1,0:T(8,128)S(1)}, u32[]{:S(2)}, u32[]{:S(2)}) collective-permute-start(f32[2,68,256]{2,1,0:T(8,128)S(1)} %get-tuple-element.31), channel_id=1, source_target_pairs={{0,1},{1,0},{2,3},{3,2},{4,5},{5,4},{6,7},{7,6},{8,9},{9,8},{10,11... | collective-permute-start | bytes 417800 | tf_op jit(solution)/shard_map/ppermute | solution.py:37
  59.1 1.1 %add_multiply_fusion = f32[16,64,256]{2,1,0:T(8,128)} fusion(f32[16,64,256]{2,1,0:T(8,128)S(1)} %get-tuple-element.24.extrap_ref.refs_2_, f32[16,64,256]{2,1,0:T(8,128)S(1)} %copy-done), kind=kLoop, calls=%fused_computation.39 | loop fusion | flops 524288 | bytes 3145728 | tf_op jit(solution)/shard_map/mul | solution.py:571
  60.3 3.5 %collective-permute-start.18 = (f32[264,128]{1,0:T(8,128)S(1)}, f32[264,128]{1,0:T(8,128)S(1)}, u32[]{:S(2)}, u32[]{:S(2)}) collective-permute-start(f32[264,128]{1,0:T(8,128)S(1)} %add.101.refs_0_), channel_id=1, source_target_pairs={{0,2},{1,3},{2,0},{3,1},{4,6},{5,7},{6,4},{7,5},{8,10},{9,11},{10,... | collective-permute-start | bytes 405512 | tf_op jit(solution)/shard_map/ppermute | solution.py:37
  63.9 0.1 pad_maximum_fusion
  64.0 1.5 %collective-permute-start.24 = (bf16[4,128,256]{2,1,0:T(8,128)(2,1)S(1)}, bf16[4,128,256]{2,1,0:T(8,128)(2,1)S(1)}, u32[]{:S(2)}, u32[]{:S(2)}) collective-permute-start(bf16[4,128,256]{2,1,0:T(8,128)(2,1)S(1)} %slice.172), channel_id=1, source_target_pairs={{0,16},{4,20},{8,24},{12,28},{16,0},{20,4},{24,8},{28,12},{1,17},{... | collective-permute-start | bytes 786440 | tf_op jit(solution)/shard_map/ppermute | solution.py:37
  65.6 1.7 %collective-permute-start.25 = (bf16[4,128,256]{2,1,0:T(8,128)(2,1)S(1)}, bf16[4,128,256]{2,1,0:T(8,128)(2,1)S(1)}, u32[]{:S(2)}, u32[]{:S(2)}) collective-permute-start(bf16[4,128,256]{2,1,0:T(8,128)(2,1)S(1)} %slice.173), channel_id=1, source_target_pairs={{0,8},{4,12},{8,0},{12,4},{16,24},{20,28},{24,16},{28,20},{1,9},{5... | collective-permute-start | bytes 786440 | tf_op jit(solution)/shard_map/ppermute | solution.py:37
  67.2 2.9 %collective-permute-done.18.refs_1_ = f32[264,128]{1,0:T(8,128)S(1)} collective-permute-done((f32[264,128]{1,0:T(8,128)S(1)}, f32[264,128]{1,0:T(8,128)S(1)}, u32[]{:S(2)}, u32[]{:S(2)}) %collective-permute-start.18) | collective-permute-done | bytes 135200 | tf_op jit(solution)/shard_map/ppermute | solution.py:37
  70.2 0.4 fusion
  70.5 0.4 collective-permute-done.24.refs_6_
  71.0 0.2 collective-permute-start.26
  71.1 0.9 %collective-permute-done.25.refs_7_ = bf16[4,128,256]{2,1,0:T(8,128)(2,1)S(1)} collective-permute-done((bf16[4,128,256]{2,1,0:T(8,128)(2,1)S(1)}, bf16[4,128,256]{2,1,0:T(8,128)(2,1)S(1)}, u32[]{:S(2)}, u32[]{:S(2)}) %collective-permute-start.25) | collective-permute-done | bytes 262176 | tf_op jit(solution)/shard_map/ppermute | solution.py:37
  72.0 1.6 %fusion.11 = f32[16,64,256]{2,1,0:T(8,128)} fusion(f32[16,64,256]{2,1,0:T(8,128)S(1)} %copy-done.5, f32[16,68,256]{2,1,0:T(8,128)S(1)} %fusion), kind=kLoop, calls=%fused_computation.26 | loop fusion | flops 2621440 | bytes 6291456 | tf_op jit(solution)/shard_map/jit(clip)/min | solution.py:576
  73.6 5.2 %rank.1 = f32[16,64,256]{2,1,0:T(8,128)} custom-call(s32[1]{0:T(128)S(6)} %copy.14.keep_ref, f32[264,128]{1,0:T(8,128)S(1)} %add.101.refs_0_, f32[264,128]{1,0:T(8,128)S(1)} %collective-permute-done.18.refs_1_, f32[16,64,256]{2,1,0:T(8,128)S(1)} %get-tuple-element.24.extrap_ref.refs_2_, f32[16,64,256]{2,1,0:T(8,128)S(1)} %copy-done.1), custom_call_target="tpu_custom_call" | custom-call | tf_op jit(solution)/shard_map/rank/pallas_call | solution.py:364
  78.9 6.7 %forward.1 = f32[1,2,1024,256]{3,2,1,0:T(8,128)} custom-call(s32[8,2,24]{2,1,0:T(2,128)S(1)} %copy-done.2, s32[2,8]{1,0:T(2,128)S(1)} %bitcast.24, bf16[1,2,24,1024,128]{4,3,2,1,0:T(8,128)(2,1)S(1)} %bitcast.22, f32[1,2,1024,256]{3,2,1,0:T(8,128)} %dual_hbm.3, bf16[1,2,1024,256]{3,2,1,0:T(8,128)(2,1)} %seen_hbm.1, f32[1,2,256]{2,1,0:T(2,128)S(1)} %copy-done.4, ...), custom_call_target="tpu_custom_call" | custom-call | tf_op jit(solution)/shard_map/forward/pallas_call | solution.py:447
  (55 shorter events, 0.4 us)
Async XLA Ops:
  1.6 11.9 %collective-permute-start = (f32[16,2,256]{2,1,0:T(2,128)S(1)}, f32[16,2,256]{2,1,0:T(2,128)S(1)}, u32[]{:S(2)}, u32[]{:S(2)}) collective-permute-start(f32[16,2,256]{2,1,0:T(2,128)S(1)} %get-tuple-element.38), channel_id=1, source_target_pairs={{4,8},{12,16},{20,24},{8,4},{16,12},{24,20},{5,9},{13,17},{21,25},... | collective-permute-start | bytes 98312 | tf_op jit(solution)/shard_map/ppermute | solution.py:50
  2.3 11.2 %collective-permute-start.1 = (f32[16,2,256]{2,1,0:T(2,128)S(1)}, f32[16,2,256]{2,1,0:T(2,128)S(1)}, u32[]{:S(2)}, u32[]{:S(2)}) collective-permute-start(f32[16,2,256]{2,1,0:T(2,128)S(1)} %get-tuple-element.39), channel_id=1, source_target_pairs={{0,4},{4,0},{8,12},{12,8},{16,20},{20,16},{24,28},{28,24},{1,5},{5... | collective-permute-start | bytes 98312 | tf_op jit(solution)/shard_map/ppermute | solution.py:37
  6.7 6.9 %copy-start.5 = (f32[16,64,256]{2,1,0:T(8,128)S(1)}, f32[16,64,256]{2,1,0:T(8,128)}, u32[]{:S(2)}) copy-start(f32[16,64,256]{2,1,0:T(8,128)} %param.11) | copy-start | bytes 3145732
  12.5 9.1 %collective-permute-start.7 = (bf16[8,256,128]{2,1,0:T(8,128)(2,1)S(1)}, bf16[8,256,128]{2,1,0:T(8,128)(2,1)S(1)}, u32[]{:S(2)}, u32[]{:S(2)}) collective-permute-start(bf16[8,256,128]{2,1,0:T(8,128)(2,1)S(1)} %get-tuple-element.23), channel_id=1, source_target_pairs={{0,4},{4,0},{8,12},{12,8},{16,20},{20,16},{24,28},{28,24},{1,5},{5... | collective-permute-start | bytes 1572872 | tf_op jit(solution)/shard_map/ppermute | solution.py:37
  13.8 7.6 %collective-permute-start.2 = (f32[2,68,256]{2,1,0:T(8,128)S(1)}, f32[2,68,256]{2,1,0:T(8,128)S(1)}, u32[]{:S(2)}, u32[]{:S(2)}) collective-permute-start(f32[2,68,256]{2,1,0:T(8,128)S(1)} %get-tuple-element.32), channel_id=1, source_target_pairs={{0,1},{1,0},{2,3},{3,2},{4,5},{5,4},{6,7},{7,6},{8,9},{9,8},{10,11... | collective-permute-start | bytes 417800 | tf_op jit(solution)/shard_map/ppermute | solution.py:37
  16.9 4.5 %collective-permute-start.3 = (f32[2,68,256]{2,1,0:T(8,128)S(1)}, f32[2,68,256]{2,1,0:T(8,128)S(1)}, u32[]{:S(2)}, u32[]{:S(2)}) collective-permute-start(f32[2,68,256]{2,1,0:T(8,128)S(1)} %get-tuple-element.33), channel_id=1, source_target_pairs={{1,2},{2,1},{5,6},{6,5},{9,10},{10,9},{13,14},{14,13},{17,18},{18,... | collective-permute-start | bytes 417800 | tf_op jit(solution)/shard_map/ppermute | solution.py:50
  17.6 13.5 %collective-permute-start.5 = (bf16[2,8,256,128]{3,2,1,0:T(8,128)(2,1)S(1)}, bf16[2,8,256,128]{3,2,1,0:T(8,128)(2,1)S(1)}, u32[]{:S(2)}, u32[]{:S(2)}) collective-permute-start(bf16[2,8,256,128]{3,2,1,0:T(8,128)(2,1)S(1)} %get-tuple-element.21), channel_id=1, source_target_pairs={{0,4},{4,0},{8,12},{12,8},{16,20},{20,16},{24,28},{28,24},{1,5},{5... | collective-permute-start | bytes 3145736 | tf_op jit(solution)/shard_map/ppermute | solution.py:37
  17.8 18.3 %collective-permute-start.4 = (bf16[8,256,128]{2,1,0:T(8,128)(2,1)S(1)}, bf16[8,256,128]{2,1,0:T(8,128)(2,1)S(1)}, u32[]{:S(2)}, u32[]{:S(2)}) collective-permute-start(bf16[8,256,128]{2,1,0:T(8,128)(2,1)S(1)} %get-tuple-element.19), channel_id=1, source_target_pairs={{0,4},{4,0},{8,12},{12,8},{16,20},{20,16},{24,28},{28,24},{1,5},{5... | collective-permute-start | bytes 1572872 | tf_op jit(solution)/shard_map/ppermute | solution.py:37
  21.7 8.2 %collective-permute-start.10 = (bf16[4,256,128]{2,1,0:T(8,128)(2,1)S(1)}, bf16[4,256,128]{2,1,0:T(8,128)(2,1)S(1)}, u32[]{:S(2)}, u32[]{:S(2)}) collective-permute-start(bf16[4,256,128]{2,1,0:T(8,128)(2,1)S(1)} %get-tuple-element.36), channel_id=1, source_target_pairs={{0,16},{4,20},{8,24},{12,28},{16,0},{20,4},{24,8},{28,12},{1,17},{... | collective-permute-start | bytes 786440 | tf_op jit(solution)/shard_map/ppermute | solution.py:37
  23.5 7.6 %collective-permute-start.8 = (bf16[4,256,128]{2,1,0:T(8,128)(2,1)S(1)}, bf16[4,256,128]{2,1,0:T(8,128)(2,1)S(1)}, u32[]{:S(2)}, u32[]{:S(2)}) collective-permute-start(bf16[4,256,128]{2,1,0:T(8,128)(2,1)S(1)} %get-tuple-element.37), channel_id=1, source_target_pairs={{0,8},{4,12},{8,0},{12,4},{16,24},{20,28},{24,16},{28,20},{1,9},{5... | collective-permute-start | bytes 786440 | tf_op jit(solution)/shard_map/ppermute | solution.py:37
  31.0 4.6 %copy-start.1 = (f32[16,64,256]{2,1,0:T(8,128)S(1)}, f32[16,64,256]{2,1,0:T(8,128)}, u32[]{:S(2)}) copy-start(f32[16,64,256]{2,1,0:T(8,128)} %refs_3_.1) | copy-start | bytes 3145732
  31.2 4.3 %copy-start = (f32[16,64,256]{2,1,0:T(8,128)S(1)}, f32[16,64,256]{2,1,0:T(8,128)}, u32[]{:S(2)}) copy-start(f32[16,64,256]{2,1,0:T(8,128)} %refs_0_.1) | copy-start | bytes 3145732
  31.3 9.2 %collective-permute-start.11 = (bf16[4,256,128]{2,1,0:T(8,128)(2,1)S(1)}, bf16[4,256,128]{2,1,0:T(8,128)(2,1)S(1)}, u32[]{:S(2)}, u32[]{:S(2)}) collective-permute-start(bf16[4,256,128]{2,1,0:T(8,128)(2,1)S(1)} %get-tuple-element.28), channel_id=1, source_target_pairs={{0,8},{4,12},{8,0},{12,4},{16,24},{20,28},{24,16},{28,20},{1,9},{5... | collective-permute-start | bytes 786440 | tf_op jit(solution)/shard_map/ppermute | solution.py:37
  31.6 9.2 %collective-permute-start.9 = (bf16[4,256,128]{2,1,0:T(8,128)(2,1)S(1)}, bf16[4,256,128]{2,1,0:T(8,128)(2,1)S(1)}, u32[]{:S(2)}, u32[]{:S(2)}) collective-permute-start(bf16[4,256,128]{2,1,0:T(8,128)(2,1)S(1)} %get-tuple-element.29), channel_id=1, source_target_pairs={{0,16},{4,20},{8,24},{12,28},{16,0},{20,4},{24,8},{28,12},{1,17},{... | collective-permute-start | bytes 786440 | tf_op jit(solution)/shard_map/ppermute | solution.py:37
  33.1 10.8 %collective-permute-start.12 = (bf16[4,256,128]{2,1,0:T(8,128)(2,1)S(1)}, bf16[4,256,128]{2,1,0:T(8,128)(2,1)S(1)}, u32[]{:S(2)}, u32[]{:S(2)}) collective-permute-start(bf16[4,256,128]{2,1,0:T(8,128)(2,1)S(1)} %get-tuple-element.26), channel_id=1, source_target_pairs={{0,16},{4,20},{8,24},{12,28},{16,0},{20,4},{24,8},{28,12},{1,17},{... | collective-permute-start | bytes 786440 | tf_op jit(solution)/shard_map/ppermute | solution.py:37
  33.8 10.1 %collective-permute-start.6 = (bf16[4,256,128]{2,1,0:T(8,128)(2,1)S(1)}, bf16[4,256,128]{2,1,0:T(8,128)(2,1)S(1)}, u32[]{:S(2)}, u32[]{:S(2)}) collective-permute-start(bf16[4,256,128]{2,1,0:T(8,128)(2,1)S(1)} %get-tuple-element.27), channel_id=1, source_target_pairs={{0,8},{4,12},{8,0},{12,4},{16,24},{20,28},{24,16},{28,20},{1,9},{5... | collective-permute-start | bytes 786440 | tf_op jit(solution)/shard_map/ppermute | solution.py:37
  44.4 10.9 %collective-permute-start.13 = (f32[16,2,256]{2,1,0:T(2,128)S(1)}, f32[16,2,256]{2,1,0:T(2,128)S(1)}, u32[]{:S(2)}, u32[]{:S(2)}) collective-permute-start(f32[16,2,256]{2,1,0:T(2,128)S(1)} %get-tuple-element.34), channel_id=1, source_target_pairs={{4,8},{12,16},{20,24},{8,4},{16,12},{24,20},{5,9},{13,17},{21,25},... | collective-permute-start | bytes 98312 | tf_op jit(solution)/shard_map/ppermute | solution.py:50
  45.1 10.2 %collective-permute-start.14 = (f32[16,2,256]{2,1,0:T(2,128)S(1)}, f32[16,2,256]{2,1,0:T(2,128)S(1)}, u32[]{:S(2)}, u32[]{:S(2)}) collective-permute-start(f32[16,2,256]{2,1,0:T(2,128)S(1)} %get-tuple-element.35), channel_id=1, source_target_pairs={{0,4},{4,0},{8,12},{12,8},{16,20},{20,16},{24,28},{28,24},{1,5},{5... | collective-permute-start | bytes 98312 | tf_op jit(solution)/shard_map/ppermute | solution.py:37
  48.7 15.4 %collective-permute-start.20 = (bf16[8,128,256]{2,1,0:T(8,128)(2,1)S(1)}, bf16[8,128,256]{2,1,0:T(8,128)(2,1)S(1)}, u32[]{:S(2)}, u32[]{:S(2)}) collective-permute-start(bf16[8,128,256]{2,1,0:T(8,128)(2,1)S(1)} %get-tuple-element.25.refs_0_), channel_id=1, source_target_pairs={{0,8},{4,12},{8,0},{12,4},{16,24},{20,28},{24,16},{28,20},{1,9},{5... | collective-permute-start | bytes 1572872 | tf_op jit(solution)/shard_map/ppermute | solution.py:37
  49.7 15.9 %collective-permute-start.22 = (bf16[8,128,256]{2,1,0:T(8,128)(2,1)S(1)}, bf16[8,128,256]{2,1,0:T(8,128)(2,1)S(1)}, u32[]{:S(2)}, u32[]{:S(2)}) collective-permute-start(bf16[8,128,256]{2,1,0:T(8,128)(2,1)S(1)} %get-tuple-element.25.refs_0_), channel_id=1, source_target_pairs={{0,16},{4,20},{8,24},{12,28},{16,0},{20,4},{24,8},{28,12},{1,17},{... | collective-permute-start | bytes 1572872 | tf_op jit(solution)/shard_map/ppermute | solution.py:37
  50.9 9.3 %collective-permute-start.17 = (f32[264,128]{1,0:T(8,128)S(1)}, f32[264,128]{1,0:T(8,128)S(1)}, u32[]{:S(2)}, u32[]{:S(2)}) collective-permute-start(f32[264,128]{1,0:T(8,128)S(1)} %gram.1), channel_id=1, source_target_pairs={{0,1},{1,0},{2,3},{3,2},{4,5},{5,4},{6,7},{7,6},{8,9},{9,8},{10,11... | collective-permute-start | bytes 405512 | tf_op jit(solution)/shard_map/ppermute | solution.py:37
  55.3 23.5 %slice-start = ((s8[12582912]{0:T(1024)(128)(4,1)}), s8[4194304]{0:T(1024)(128)(4,1)S(1)}, s32[]{:S(2)}) async-start(s8[12582912]{0:T(1024)(128)(4,1)} %bitcast.21), calls=%async_computation | async-start | bytes 8388608
  55.5 4.8 %collective-permute-start.15 = (f32[2,68,256]{2,1,0:T(8,128)S(1)}, f32[2,68,256]{2,1,0:T(8,128)S(1)}, u32[]{:S(2)}, u32[]{:S(2)}) collective-permute-start(f32[2,68,256]{2,1,0:T(8,128)S(1)} %get-tuple-element.30), channel_id=1, source_target_pairs={{1,2},{2,1},{5,6},{6,5},{9,10},{10,9},{13,14},{14,13},{17,18},{18,... | collective-permute-start | bytes 417800 | tf_op jit(solution)/shard_map/ppermute | solution.py:50
  56.5 7.3 %collective-permute-start.16 = (f32[2,68,256]{2,1,0:T(8,128)S(1)}, f32[2,68,256]{2,1,0:T(8,128)S(1)}, u32[]{:S(2)}, u32[]{:S(2)}) collective-permute-start(f32[2,68,256]{2,1,0:T(8,128)S(1)} %get-tuple-element.31), channel_id=1, source_target_pairs={{0,1},{1,0},{2,3},{3,2},{4,5},{5,4},{6,7},{7,6},{8,9},{9,8},{10,11... | collective-permute-start | bytes 417800 | tf_op jit(solution)/shard_map/ppermute | solution.py:37
  60.3 18.5 %collective-permute-start.19 = (bf16[8,128,256]{2,1,0:T(8,128)(2,1)S(1)}, bf16[8,128,256]{2,1,0:T(8,128)(2,1)S(1)}, u32[]{:S(2)}, u32[]{:S(2)}) collective-permute-start(bf16[8,128,256]{2,1,0:T(8,128)(2,1)S(1)} %get-tuple-element.25.refs_0_), channel_id=1, source_target_pairs={{0,4},{4,0},{8,12},{12,8},{16,20},{20,16},{24,28},{28,24},{1,5},{5... | collective-permute-start | bytes 1572872 | tf_op jit(solution)/shard_map/ppermute | solution.py:37
  60.3 9.9 %collective-permute-start.18 = (f32[264,128]{1,0:T(8,128)S(1)}, f32[264,128]{1,0:T(8,128)S(1)}, u32[]{:S(2)}, u32[]{:S(2)}) collective-permute-start(f32[264,128]{1,0:T(8,128)S(1)} %add.101.refs_0_), channel_id=1, source_target_pairs={{0,2},{1,3},{2,0},{3,1},{4,6},{5,7},{6,4},{7,5},{8,10},{9,11},{10,... | collective-permute-start | bytes 405512 | tf_op jit(solution)/shard_map/ppermute | solution.py:37
  63.9 15.0 %slice-start.1 = ((s8[12582912]{0:T(1024)(128)(4,1)}), s8[4194304]{0:T(1024)(128)(4,1)S(1)}, s32[]{:S(2)}) async-start(s8[12582912]{0:T(1024)(128)(4,1)} %bitcast.21), calls=%async_computation.1 | async-start | bytes 8388608
  64.0 6.9 %collective-permute-start.24 = (bf16[4,128,256]{2,1,0:T(8,128)(2,1)S(1)}, bf16[4,128,256]{2,1,0:T(8,128)(2,1)S(1)}, u32[]{:S(2)}, u32[]{:S(2)}) collective-permute-start(bf16[4,128,256]{2,1,0:T(8,128)(2,1)S(1)} %slice.172), channel_id=1, source_target_pairs={{0,16},{4,20},{8,24},{12,28},{16,0},{20,4},{24,8},{28,12},{1,17},{... | collective-permute-start | bytes 786440 | tf_op jit(solution)/shard_map/ppermute | solution.py:37
  65.6 6.4 %collective-permute-start.25 = (bf16[4,128,256]{2,1,0:T(8,128)(2,1)S(1)}, bf16[4,128,256]{2,1,0:T(8,128)(2,1)S(1)}, u32[]{:S(2)}, u32[]{:S(2)}) collective-permute-start(bf16[4,128,256]{2,1,0:T(8,128)(2,1)S(1)} %slice.173), channel_id=1, source_target_pairs={{0,8},{4,12},{8,0},{12,4},{16,24},{20,28},{24,16},{28,20},{1,9},{5... | collective-permute-start | bytes 786440 | tf_op jit(solution)/shard_map/ppermute | solution.py:37
  67.2 11.6 %collective-permute-start.21 = (bf16[8,128,256]{2,1,0:T(8,128)(2,1)S(1)}, bf16[8,128,256]{2,1,0:T(8,128)(2,1)S(1)}, u32[]{:S(2)}, u32[]{:S(2)}) collective-permute-start(bf16[8,128,256]{2,1,0:T(8,128)(2,1)S(1)} %collective-permute-done.20.refs_2_), channel_id=1, source_target_pairs={{0,4},{4,0},{8,12},{12,8},{16,20},{20,16},{24,28},{28,24},{1,5},{5... | collective-permute-start | bytes 1572872 | tf_op jit(solution)/shard_map/ppermute | solution.py:37
  70.1 8.7 %collective-permute-start.23 = (bf16[8,128,256]{2,1,0:T(8,128)(2,1)S(1)}, bf16[8,128,256]{2,1,0:T(8,128)(2,1)S(1)}, u32[]{:S(2)}, u32[]{:S(2)}) collective-permute-start(bf16[8,128,256]{2,1,0:T(8,128)(2,1)S(1)} %collective-permute-done.22.refs_4_), channel_id=1, source_target_pairs={{0,4},{4,0},{8,12},{12,8},{16,20},{20,16},{24,28},{28,24},{1,5},{5... | collective-permute-start | bytes 1572872 | tf_op jit(solution)/shard_map/ppermute | solution.py:37
  70.5 8.3 %slice-start.2 = ((s8[12582912]{0:T(1024)(128)(4,1)}), s8[4194304]{0:T(1024)(128)(4,1)S(1)}, s32[]{:S(2)}) async-start(s8[12582912]{0:T(1024)(128)(4,1)} %bitcast.21), calls=%async_computation.2 | async-start | bytes 8388608
  71.0 7.8 %collective-permute-start.26 = (bf16[4,128,256]{2,1,0:T(8,128)(2,1)S(1)}, bf16[4,128,256]{2,1,0:T(8,128)(2,1)S(1)}, u32[]{:S(2)}, u32[]{:S(2)}) collective-permute-start(bf16[4,128,256]{2,1,0:T(8,128)(2,1)S(1)} %collective-permute-done.24.refs_6_), channel_id=1, source_target_pairs={{0,4},{4,0},{8,12},{12,8},{16,20},{20,16},{24,28},{28,24},{1,5},{5... | collective-permute-start | bytes 786440 | tf_op jit(solution)/shard_map/ppermute | solution.py:37
  72.0 6.8 %collective-permute-start.27 = (bf16[4,128,256]{2,1,0:T(8,128)(2,1)S(1)}, bf16[4,128,256]{2,1,0:T(8,128)(2,1)S(1)}, u32[]{:S(2)}, u32[]{:S(2)}) collective-permute-start(bf16[4,128,256]{2,1,0:T(8,128)(2,1)S(1)} %collective-permute-done.25.refs_7_), channel_id=1, source_target_pairs={{0,4},{4,0},{8,12},{12,8},{16,20},{20,16},{24,28},{28,24},{1,5},{5... | collective-permute-start | bytes 786440 | tf_op jit(solution)/shard_map/ppermute | solution.py:37
  73.6 5.3 %copy-start.2 = (s32[8,2,24]{2,1,0:T(2,128)S(1)}, s32[8,2,24]{2,1,0:T(2,128)}, u32[]{:S(2)}) copy-start(s32[8,2,24]{2,1,0:T(2,128)} %tiles) | copy-start | bytes 4612
  73.6 5.3 %copy-start.3 = (s32[8,2]{0,1:T(2,128)S(1)}, s32[8,2]{0,1:T(2,128)}, u32[]{:S(2)}) copy-start(s32[8,2]{0,1:T(2,128)} %param.18) | copy-start | bytes 196
  73.6 5.3 %copy-start.4 = (f32[1,2,256]{2,1,0:T(2,128)S(1)}, f32[1,2,256]{2,1,0:T(2,128)}, u32[]{:S(2)}) copy-start(f32[1,2,256]{2,1,0:T(2,128)} %radius_ref.1) | copy-start | bytes 6148
